TPU v7x, 256 devices: a whole 4x4x8 slice. The times are simulated.
256 devices in a mesh: dp: 4 (over y), seq: 64 (over z, x, core).
Axes of the slice: x: 4, y: 4, z: 8, core: 2. Of those that a mesh axis runs over, the one named last changes fastest.
Arguments:
- query_tokens: bfloat16 [131072, 1024], P(('dp', 'seq')), parts along dimension 0, may hold values from -6 to 6
- key_tokens: bfloat16 [131072, 1024], P(('dp', 'seq')), parts along dimension 0, may hold values from -6 to 6
- value_tokens: bfloat16 [131072, 1024], P(('dp', 'seq')), parts along dimension 0, may hold values from -6 to 6
- gate_tokens: bfloat16 [131072, 1024], P(('dp', 'seq')), parts along dimension 0, may hold values from -6 to 6
- filter_taps: float32 [27, 1024], replicated, may hold values from -1.25 to 1.25
- selected: int32 [2048, 8, 8], P(('dp', 'seq')), parts along dimension 0, may hold values from 0 to 511, as said below
- cotangent: bfloat16 [131072, 1024], P(('dp', 'seq')), parts along dimension 0, may hold values from -6 to 6
Outputs:
- attended: bfloat16 [131072, 1024], P(('dp', 'seq')), parts along dimension 0
- query_gradient: bfloat16 [131072, 1024], P(('dp', 'seq')), parts along dimension 0
- key_gradient: bfloat16 [131072, 1024], P(('dp', 'seq')), parts along dimension 0
- value_gradient: bfloat16 [131072, 1024], P(('dp', 'seq')), parts along dimension 0
- gate_gradient: bfloat16 [131072, 1024], P(('dp', 'seq')), parts along dimension 0
- filter_gradient: float32 [108, 1024], P('dp'), parts along dimension 0
There are 4 independent parts, one for each index of `dp`. A program takes and returns all parts, laid end to end along the dimension named above; an argument that names none is the same for every part. Nothing has to cross between parts.
Inputs may be any that keep to these rules, and one draw needn't show every extreme that they name: `selected`: for each query cube and head the 8 entries are distinct. Over the 8 query cubes of one device, the pairs of key cube and head that lie on other devices number exactly 96, at most 3 of them on any one other device; in every draw one device receives exactly 3 such pairs from every other device.
All inputs are finite; a program needn't handle non-finite values.
Results may differ from a plain program's by a relative error of at most 0.0075.
The roundings to bfloat16 on the way count: a program that leaves them out, or rounds other values in their place, can miss the bound.
Values may be sent and summed in bfloat16 or wider, within the bound.
No kernel may reach another device: no remote copies, remote signals or barrier semaphores. Data moves between devices by JAX's collectives and lax.ppermute only.
A program may use at most 192 MiB of HBM per device.

v0:
```python
import jax
import jax.numpy as jnp
from jax import lax
from jax.sharding import PartitionSpec as P

HEAD_DIM = 128
HEADS = 8
SLABS = 4
POOL = 12


def from_partner(block, axis, apart):
    count = lax.axis_size(axis)
    route = []
    for low in range(count):
        high = low | 1 << apart
        if high != low and high < count:
            route += [(low, high), (high, low)]
    return lax.ppermute(block, axis, route)


def with_halo(cells, sides, width):
    for axis, dim in sides:
        count = lax.axis_size(axis)
        head = lax.slice_in_dim(cells, 0, width, axis=dim)
        tail = lax.slice_in_dim(cells, cells.shape[dim] - width, cells.shape[dim], axis=dim)
        cells = jnp.concatenate(
            [
                lax.ppermute(tail, axis, [(i, (i + 1) % count) for i in range(count)]),
                cells,
                lax.ppermute(head, axis, [((i + 1) % count, i) for i in range(count)]),
            ],
            axis=dim,
        )
    return cells


def passed_along(value, axis, steps):
    count = lax.axis_size(axis)
    pairs = [(source, (source + steps) % count) for source in range(count)]
    return lax.ppermute(value, axis, pairs)


def shortened(shard):

    def short(part):
        return part.astype(jnp.bfloat16) if part.dtype == jnp.float32 else part

    return jax.tree.map(short, shard)


def to_blocks(tokens):
    cube_count = tokens.shape[0] // 64
    return tokens.reshape(cube_count, 64, HEADS, HEAD_DIM).transpose(0, 2, 1, 3)


def from_blocks(blocks):
    cube_count = blocks.shape[0]
    return blocks.transpose(0, 2, 1, 3).reshape(cube_count * 64, HEADS * HEAD_DIM)


def to_lattice(tokens):
    channels = tokens.shape[1]
    cube_count = tokens.shape[0] // 64
    lattice = tokens.reshape(cube_count, 4, 4, 4, channels).transpose(1, 2, 0, 3, 4)
    return lattice.reshape(4, 4, cube_count * 4, channels)


def from_lattice(lattice):
    channels = lattice.shape[3]
    cube_count = lattice.shape[2] // 4
    tokens = lattice.reshape(4, 4, cube_count, 4, channels).transpose(2, 0, 1, 3, 4)
    return tokens.reshape(cube_count * 64, channels)


def side_columns(lattice, edge, col_half):
    blank = jnp.zeros_like(edge)
    return jnp.concatenate(
        [jnp.where(col_half == 1, edge, blank), lattice, jnp.where(col_half == 0, edge, blank)],
        axis=2,
    )


def clear_rims(extended, row_band, band_count):
    blank = jnp.zeros_like(extended[:, :1])
    upper = jnp.where(row_band > 0, extended[:, :1], blank)
    lower = jnp.where(row_band < band_count - 1, extended[:, -1:], blank)
    return jnp.concatenate([upper, extended[:, 1:-1], lower], axis=1)


def convolve_values(framed, filter_taps):
    frames = framed.shape[0] - 2
    height = framed.shape[1] - 2
    breadth = framed.shape[2] - 2
    totaled_sum = jnp.zeros((frames, height, breadth, framed.shape[3]), jnp.float32)
    for back_step in range(3):
        for row_step in (-1, 0, 1):
            for col_step in (-1, 0, 1):
                tap_index = back_step * 9 + (row_step + 1) * 3 + col_step + 1
                shifted = framed[
                    2 - back_step : 2 - back_step + frames,
                    1 + row_step : 1 + row_step + height,
                    1 + col_step : 1 + col_step + breadth,
                ]
                totaled_sum = totaled_sum + filter_taps[tap_index] * shifted.astype(jnp.float32)
    return totaled_sum


def convolve_back(grad_space, framed, filter_taps):
    frames = grad_space.shape[0] - 2
    height = grad_space.shape[1] - 2
    breadth = grad_space.shape[2] - 2
    inner_grad = grad_space[:frames, 1:-1, 1:-1]
    totaled_sum = jnp.zeros(inner_grad.shape, jnp.float32)
    tap_rows = []
    for back_step in range(3):
        for row_step in (-1, 0, 1):
            for col_step in (-1, 0, 1):
                tap_index = back_step * 9 + (row_step + 1) * 3 + col_step + 1
                totaled_sum = (
                    totaled_sum
                    + filter_taps[tap_index]
                    * grad_space[
                        back_step : back_step + frames,
                        1 - row_step : 1 - row_step + height,
                        1 - col_step : 1 - col_step + breadth,
                    ]
                )
                shifted = framed[
                    2 - back_step : 2 - back_step + frames,
                    1 + row_step : 1 + row_step + height,
                    1 + col_step : 1 + col_step + breadth,
                ]
                tap_rows.append(jnp.sum(inner_grad * shifted.astype(jnp.float32), axis=(0, 1, 2)))
    return (totaled_sum, jnp.stack(tap_rows))


def pool_cubes(tokens):
    return jnp.mean(
        tokens.astype(jnp.float32).reshape(tokens.shape[0] // 64, 64, tokens.shape[1]), axis=1
    )


def separate_heads(rows):
    return rows.reshape(rows.shape[0], HEADS, HEAD_DIM)


def spread(per_cube):
    cube_count = per_cube.shape[0]
    return jnp.broadcast_to(per_cube[:, None, :], (cube_count, 64, per_cube.shape[1])).reshape(
        cube_count * 64, per_cube.shape[1]
    )


def coarse_forward(averaged_query, averaged_key, averaged_value, logit_scale):
    logit_matrix = (
        jnp.einsum(
            "agt,ogt->gao",
            separate_heads(averaged_query),
            separate_heads(averaged_key),
            preferred_element_type=jnp.float32,
        )
        * logit_scale
    )
    row_max = jnp.max(logit_matrix, axis=2, keepdims=True)
    exponent = jnp.exp(logit_matrix - row_max)
    weights = exponent / jnp.sum(exponent, axis=2, keepdims=True)
    rounded_result = weights.astype(jnp.bfloat16)
    blended_output = jnp.einsum(
        "clx,xcu->lcu",
        rounded_result,
        separate_heads(averaged_value),
        preferred_element_type=jnp.float32,
    )
    return (
        weights,
        rounded_result,
        blended_output.reshape(blended_output.shape[0], HEADS * HEAD_DIM),
    )


def coarse_delta(averaged_gradient, coarse_out):
    return jnp.sum(
        separate_heads(averaged_gradient).astype(jnp.float32) * separate_heads(coarse_out), axis=2
    ).T


def score_grads(weights, averaged_gradient, averaged_value, row_delta):
    weight_gradient_total = jnp.einsum(
        "agt,ogt->gao",
        separate_heads(averaged_gradient),
        separate_heads(averaged_value),
        preferred_element_type=jnp.float32,
    )
    return (weights * (weight_gradient_total - row_delta[:, :, None])).astype(jnp.bfloat16)


def query_side(logit_gradient, averaged_key, logit_scale):
    totaled_sum = (
        jnp.einsum(
            "clx,xcu->lcu",
            logit_gradient,
            separate_heads(averaged_key),
            preferred_element_type=jnp.float32,
        )
        * logit_scale
    )
    return totaled_sum.reshape(totaled_sum.shape[0], HEADS * HEAD_DIM)


def key_side(logit_gradient, rounded_result, averaged_query, averaged_gradient, logit_scale):
    key_portion = (
        jnp.einsum(
            "opk,poe->koe",
            logit_gradient,
            separate_heads(averaged_query),
            preferred_element_type=jnp.float32,
        )
        * logit_scale
    )
    value_portion = jnp.einsum(
        "opk,poe->koe",
        rounded_result,
        separate_heads(averaged_gradient),
        preferred_element_type=jnp.float32,
    )
    key_count = key_portion.shape[0]
    return jnp.concatenate(
        [key_portion.reshape(key_count, -1), value_portion.reshape(key_count, -1)], axis=1
    )


def attend_cube(table_key, table_value, query_cube, grad_cube, row_cube, logit_scale):
    head_count, pick_count = row_cube.shape
    flat_rows = row_cube.reshape(-1)
    key_rows = table_key[flat_rows].reshape(head_count, pick_count * 64, HEAD_DIM)
    value_rows = table_value[flat_rows].reshape(head_count, pick_count * 64, HEAD_DIM)
    logit_matrix = (
        jnp.einsum("hqd,hkd->hqk", query_cube, key_rows, preferred_element_type=jnp.float32)
        * logit_scale
    )
    row_max = jnp.max(logit_matrix, axis=2, keepdims=True)
    exponent = jnp.exp(logit_matrix - row_max)
    weights = exponent / jnp.sum(exponent, axis=2, keepdims=True)
    rounded_result = weights.astype(jnp.bfloat16)
    fine_out = jnp.einsum(
        "hqk,hkd->hqd", rounded_result, value_rows, preferred_element_type=jnp.float32
    )
    row_delta = jnp.sum(grad_cube.astype(jnp.float32) * fine_out, axis=2, keepdims=True)
    weight_gradient_total = jnp.einsum(
        "hqd,hkd->hqk", grad_cube, value_rows, preferred_element_type=jnp.float32
    )
    logit_gradient = (weights * (weight_gradient_total - row_delta)).astype(jnp.bfloat16)
    query_grad = (
        jnp.einsum("hqk,hkd->hqd", logit_gradient, key_rows, preferred_element_type=jnp.float32)
        * logit_scale
    )
    key_grad = (
        jnp.einsum("hqk,hqd->hkd", logit_gradient, query_cube, preferred_element_type=jnp.float32)
        * logit_scale
    )
    value_grad = jnp.einsum(
        "hqk,hqd->hkd", rounded_result, grad_cube, preferred_element_type=jnp.float32
    )
    return (
        fine_out,
        query_grad,
        key_grad.reshape(head_count * pick_count, 64, HEAD_DIM),
        value_grad.reshape(head_count * pick_count, 64, HEAD_DIM),
    )


def shards(query_tokens, key_tokens, value_tokens, gate_tokens, filter_taps, selected, cotangent):
    devices = lax.axis_size("seq")
    device_index = lax.axis_index("seq")
    cube_count = query_tokens.shape[0] // 64
    pair_count = cube_count * HEADS
    channels = HEADS * HEAD_DIM
    capacity = max(3, 2 * HEADS * POOL // (devices - 1))
    logit_scale = HEAD_DIM ** (-0.5)
    band_count = devices // (2 * SLABS)
    rotated = (device_index + 2 * band_count + band_count // 2) % devices
    row_band = rotated % band_count
    slab_index = rotated // band_count % SLABS
    col_half = rotated // (devices // 2)
    col_bit = devices.bit_length() - 2
    lattice = to_lattice(value_tokens)
    value_edge = from_partner(
        jnp.where(col_half == 0, lattice[:, :, -1:], lattice[:, :, :1]), "seq", col_bit
    )
    value_wide = side_columns(lattice, value_edge, col_half)
    value_tall = clear_rims(with_halo(value_wide, (("seq", 1),), 1), row_band, band_count)
    prior_frames = passed_along(value_tall[-2:], "seq", band_count)
    prior_frames = jnp.where(slab_index > 0, prior_frames, jnp.zeros_like(prior_frames))
    framed = jnp.concatenate([prior_frames, value_tall], axis=0)
    filtered = from_lattice(convolve_values(framed, filter_taps)).astype(jnp.bfloat16)
    averaged_query = pool_cubes(query_tokens).astype(jnp.bfloat16)
    averaged_key = pool_cubes(key_tokens).astype(jnp.bfloat16)
    averaged_value = pool_cubes(filtered).astype(jnp.bfloat16)
    gated = cotangent.astype(jnp.float32) * gate_tokens.astype(jnp.float32)
    averaged_gradient = jnp.sum(gated.reshape(cube_count, 64, channels), axis=1).astype(
        jnp.bfloat16
    )
    all_keys, all_values = (
        lax.all_gather(averaged_key, "seq", axis=0, tiled=True),
        lax.all_gather(averaged_value, "seq", axis=0, tiled=True),
    )
    weights, rounded_result, coarse_out = coarse_forward(
        averaged_query, all_keys, all_values, logit_scale
    )
    row_delta = coarse_delta(averaged_gradient, coarse_out)
    logit_gradient = score_grads(weights, averaged_gradient, all_values, row_delta)
    coarse_query = query_side(logit_gradient, all_keys, logit_scale)
    shares = lax.psum_scatter(
        key_side(logit_gradient, rounded_result, averaged_query, averaged_gradient, logit_scale),
        "seq",
        scatter_dimension=0,
        tiled=True,
    )
    owner_device = selected // cube_count
    pair_index = selected % cube_count * HEADS + jnp.arange(HEADS, dtype=jnp.int32)[None, :, None]
    remote_flat = (owner_device != device_index).reshape(-1)
    pair_codes = (owner_device * pair_count + pair_index).reshape(-1)
    matches = (
        pair_codes[:, None] == jnp.arange(devices * pair_count, dtype=jnp.int32)[None, :]
    ) & remote_flat[:, None]
    present = jnp.any(matches, axis=0).reshape(devices, pair_count).astype(jnp.int32)
    slot_rank = jnp.cumsum(present, axis=1) - present
    in_slot = (slot_rank[:, :, None] == jnp.arange(capacity, dtype=jnp.int32)[None, None, :]) & (
        present[:, :, None] > 0
    )
    requests = jnp.sum(
        in_slot.astype(jnp.int32) * jnp.arange(pair_count, dtype=jnp.int32)[None, :, None], axis=1
    ).reshape(-1)
    slot_of = jnp.sum(matches.astype(jnp.int32) * slot_rank.reshape(-1)[None, :], axis=1)
    table_row = jnp.where(
        remote_flat,
        pair_count + owner_device.reshape(-1) * capacity + slot_of,
        pair_index.reshape(-1),
    ).reshape(cube_count, HEADS, -1)
    asked_pairs = lax.all_to_all(requests, "seq", split_axis=0, concat_axis=0, tiled=True)
    own_keys = to_blocks(key_tokens).reshape(pair_count, 64, HEAD_DIM)
    own_values = to_blocks(filtered).reshape(pair_count, 64, HEAD_DIM)
    fetched_keys, fetched_values = (
        lax.all_to_all(own_keys[asked_pairs], "seq", split_axis=0, concat_axis=0, tiled=True),
        lax.all_to_all(own_values[asked_pairs], "seq", split_axis=0, concat_axis=0, tiled=True),
    )
    table_key = jnp.concatenate([own_keys, fetched_keys], axis=0)
    table_value = jnp.concatenate([own_values, fetched_values], axis=0)

    def scan_step(accumulated, inputs):
        key_acc, value_acc = accumulated
        query_cube, grad_cube, row_cube = inputs
        fine_out, query_grad, key_grad, value_grad = attend_cube(
            table_key, table_value, query_cube, grad_cube, row_cube, logit_scale
        )
        flat_rows = row_cube.reshape(-1)
        return (
            (key_acc.at[flat_rows].add(key_grad), value_acc.at[flat_rows].add(value_grad)),
            (fine_out, query_grad),
        )

    zeros_table = jnp.zeros((table_key.shape[0], 64, HEAD_DIM), jnp.float32)
    (key_acc, value_acc), (fine_out, fine_query) = lax.scan(
        scan_step,
        (zeros_table, zeros_table),
        (to_blocks(query_tokens), to_blocks(cotangent), table_row),
    )
    returned_keys, returned_values = (
        lax.all_to_all(
            key_acc[pair_count:].astype(jnp.bfloat16),
            "seq",
            split_axis=0,
            concat_axis=0,
            tiled=True,
        ).astype(jnp.float32),
        lax.all_to_all(
            value_acc[pair_count:].astype(jnp.bfloat16),
            "seq",
            split_axis=0,
            concat_axis=0,
            tiled=True,
        ).astype(jnp.float32),
    )
    key_grad = key_acc[:pair_count].at[asked_pairs].add(returned_keys)
    value_grad = value_acc[:pair_count].at[asked_pairs].add(returned_values)
    coarse_tokens = spread(coarse_out)
    attended = (from_blocks(fine_out) + gate_tokens.astype(jnp.float32) * coarse_tokens).astype(
        jnp.bfloat16
    )
    gate_gradient = (cotangent.astype(jnp.float32) * coarse_tokens).astype(jnp.bfloat16)
    query_gradient = (from_blocks(fine_query) + spread(coarse_query) / 64.0).astype(jnp.bfloat16)
    fine_key = from_blocks(key_grad.reshape(cube_count, HEADS, 64, HEAD_DIM))
    key_gradient = (fine_key + spread(shares[:, :channels]) / 64.0).astype(jnp.bfloat16)
    fine_value = from_blocks(value_grad.reshape(cube_count, HEADS, 64, HEAD_DIM))
    filtered_grad = fine_value + spread(shares[:, channels:]) / 64.0
    grad_lattice = to_lattice(filtered_grad)
    grad_edge = from_partner(
        jnp.where(col_half == 0, grad_lattice[:, :, -1:], grad_lattice[:, :, :1]).astype(
            jnp.bfloat16
        ),
        "seq",
        col_bit,
    ).astype(jnp.float32)
    grad_wide = side_columns(grad_lattice, grad_edge, col_half)
    grad_tall = clear_rims(with_halo(grad_wide, (("seq", 1),), 1), row_band, band_count)
    next_frames = passed_along(shortened(grad_tall[:2]), "seq", -band_count)
    next_frames = jnp.where(slab_index < SLABS - 1, next_frames, jnp.zeros_like(next_frames))
    value_lattice, tap_grads = convolve_back(
        jnp.concatenate([grad_tall, next_frames], axis=0), framed, filter_taps
    )
    value_gradient = from_lattice(value_lattice).astype(jnp.bfloat16)
    filter_gradient = lax.psum(tap_grads, "seq")
    return (attended, query_gradient, key_gradient, value_gradient, gate_gradient, filter_gradient)


def solution(mesh):
    return jax.shard_map(
        shards,
        mesh=mesh,
        in_specs=(
            P(("dp", "seq"), None),
            P(("dp", "seq"), None),
            P(("dp", "seq"), None),
            P(("dp", "seq"), None),
            P(),
            P(("dp", "seq"), None, None),
            P(("dp", "seq"), None),
        ),
        out_specs=(
            P(("dp", "seq"), None),
            P(("dp", "seq"), None),
            P(("dp", "seq"), None),
            P(("dp", "seq"), None),
            P(("dp", "seq"), None),
            P("dp", None),
        ),
        check_vma=False,
    )
```

profile of v0, /device:TPU:1, one launch (start us, length us, event | category | flops | bytes accessed | tf_op | source)
XLA Modules:
  0.0 1285.3 jit_solution(3060292123169904972)
XLA Ops:
  12.6 13.0 %all-to-all-start = ((s32[64,3,1]{1,2,0:T(1,128)}), s32[64,3,1]{1,2,0:T(1,128)S(1)}, u32[]{:S(2)}, u32[]{:S(2)}) async-start(s32[64,3,1]{1,2,0:T(1,128)} %copy.125), calls=%async_computation | async-start | bytes 65536 | tf_op jit(solution)/shard_map/all_to_all | solution.py:341
  48.9 10.7 collective-permute-done.2
  67.3 57.4 %collective-permute-done.3 = bf16[2,6,34,1024]{3,0,2,1:T(2,128)(2,1)S(1)} collective-permute-done((bf16[2,6,34,1024]{3,0,2,1:T(2,128)(2,1)S(1)}, bf16[2,6,34,1024]{3,0,2,1:T(2,128)(2,1)S(1)}, u32[]{:S(2)}, u32[]{:S(2)}) %collective-permute-start.3) | collective-permute-done | bytes 835616 | tf_op jit(solution)/shard_map/ppermute | solution.py:41
  127.9 16.9 %convert_reduce_fusion.2 = (f32[32,1024]{1,0:T(8,128)}, bf16[4,4,32,1024]{3,1,2,0:T(4,128)(2,1)S(1)}) fusion(bf16[6,6,34,1024]{3,1,2,0:T(8,128)(2,1)S(1)} %maximum_maximum_fusion.1, f32[1024]{0:T(1024)S(1)} %bitcast.326, f32[1024]{0:T(1024)S(1)} %bitcast.328, f32[1024]{0:T(1024)S(1)} %bitcast.332, f32[1024]{0:T(1024)S(1)} %bitcast.334, ...), kind=kLoop, calls=%fused_computation.231 | loop fusion | flops 44531712 | bytes 27570176 | tf_op jit(solution)/shard_map/reduce_sum | solution.py:139
  151.2 20.9 %all-to-all-start.2 = ((bf16[192,64,128]{2,1,0:T(8,128)(2,1)}), bf16[192,64,128]{2,1,0:T(8,128)(2,1)}, u32[]{:S(2)}, u32[]{:S(2)}) async-start(bf16[192,64,128]{2,1,0:T(8,128)(2,1)} %gather_fusion.3), calls=%async_computation.2 | async-start | bytes 6291456 | tf_op jit(solution)/shard_map/all_to_all | solution.py:346
  184.4 62.2 %all-to-all-done.2 = bf16[192,64,128]{2,1,0:T(8,128)(2,1)} async-done(((bf16[192,64,128]{2,1,0:T(8,128)(2,1)}), bf16[192,64,128]{2,1,0:T(8,128)(2,1)}, u32[]{:S(2)}, u32[]{:S(2)}) %all-to-all-start.2) | async-done | bytes 3145760 | tf_op jit(solution)/shard_map/all_to_all | solution.py:346
  259.7 402.7 %while.16 = (s32[]{:T(128)}, f32[256,64,128]{2,1,0:T(8,128)}, f32[256,64,128]{2,1,0:T(8,128)}, f32[8,8,64,128]{3,2,1,0:T(8,128)}, f32[8,8,64,128]{3,2,1,0:T(8,12...) while((s32[]{:T(128)}, f32[256,64,128]{2,1,0:T(8,128)}, ...), condition=%wide.region_10.11_spmd, body=%wide.region_4.10_spmd.sunk | while | flops 407899328 | bytes 42634256 | solution.py:364
  289.3 10.4 scatter_fusion
  299.7 10.4 scatter_fusion.1
  350.1 10.4 scatter_fusion.1
  390.0 10.4 scatter_fusion
  450.7 10.4 scatter_fusion.1
  501.0 10.4 scatter_fusion.1
  591.3 10.4 scatter_fusion
  601.7 10.4 scatter_fusion.1
  641.7 10.4 scatter_fusion
  652.1 10.4 scatter_fusion.1
  689.3 69.4 %all-gather.3.cloned.1.call-done = bf16[512,1024]{1,0:T(8,128)(2,1)} async-done(((bf16[8,1024]{1,0:T(8,128)(2,1)}), bf16[512,1024]{1,0:T(8,128)(2,1)}) %all-gather.3.cloned.1.call-update) | async-done | bytes 1048592 | tf_op jit(solution)/shard_map/all_gather | solution.py:306
  785.2 214.0 %all-reduce.6.cloned.1.call-done = f32[512,2048]{0,1:T(8,128)} async-done(((f32[512,2048]{0,1:T(8,128)}), f32[512,2048]{0,1:T(8,128)}) %all-reduce.6.cloned.1.call-update) | async-done | bytes 4194320
  1012.7 29.6 %scatter_fusion.3 = f32[64,64,128]{2,1,0:T(8,128)} fusion(f32[64,64,128]{2,1,0:T(8,128)} %slice.418, s32[192]{0:T(256)S(1)} %bitcast.396, f32[192,64,128]{2,1,0:T(8,128)} %convert_element_type.296), kind=kCustom, calls=%fused_computation.7 | custom fusion | flops 1572864 | bytes 18875136 | tf_op jit(solution)/shard_map/scatter-add | solution.py:386
  1075.5 12.3 fusion.69
  1107.6 20.1 %scatter_fusion.2 = f32[64,64,128]{2,1,0:T(8,128)S(1)} fusion(f32[64,64,128]{2,1,0:T(8,128)S(1)} %copy-done.3, s32[192]{0:T(256)S(1)} %bitcast.397, f32[192,64,128]{2,1,0:T(8,128)} %convert_element_type.294), kind=kCustom, calls=%fused_computation.6 | custom fusion | flops 1572864 | bytes 18875136 | tf_op jit(solution)/shard_map/scatter-add | solution.py:385
  1140.9 36.2 %fusion.76 = bf16[4,4,32,1024]{3,1,2,0:T(4,128)(2,1)S(1)} fusion(f32[6,6,34,1024]{3,1,2,0:T(8,128)} %pad_maximum_fusion, f32[4,5,34,1024]{3,1,2,0:T(8,128)} %get-tuple-element.179, f32[4,4,32,1024]{3,1,2,0:T(4,128)S(1)} %bitcast.275, f32[4,4,1,1024]{3,1,2,0:T(4,128)S(1)} %get-tuple-element.215, f32[4,4,1,1024]{3,1,2,0:T(4,128)S(1)} %get-tuple-element.216, ...), kind=kLoop, calls=%fused_computation.171 | loop fusion | flops 29360128 | bytes 53719040 | tf_op jit(solution)/shard_map/convert_element_type | solution.py:412
  1178.8 97.9 %all-reduce.4.cloned.1.call-done = f32[27,1024]{1,0:T(8,128)} async-done(((f32[27,1024]{1,0:T(8,128)}), f32[27,1024]{1,0:T(8,128)}) %all-reduce.4.cloned.1.call-update) | async-done | bytes 110608 | tf_op jit(solution)/shard_map/psum | solution.py:413
  (539 shorter events, 504.0 us)
Async XLA Ops:
  12.6 22.3 %all-to-all-start = ((s32[64,3,1]{1,2,0:T(1,128)}), s32[64,3,1]{1,2,0:T(1,128)S(1)}, u32[]{:S(2)}, u32[]{:S(2)}) async-start(s32[64,3,1]{1,2,0:T(1,128)} %copy.125), calls=%async_computation | async-start | bytes 65536 | tf_op jit(solution)/shard_map/all_to_all | solution.py:341
  27.8 17.0 %collective-permute-start = (bf16[4,4,1,1024]{3,1,2,0:T(4,128)(2,1)S(1)}, bf16[4,4,1,1024]{3,1,2,0:T(4,128)(2,1)S(1)}, u32[]{:S(2)}, u32[]{:S(2)}) collective-permute-start(bf16[4,4,1,1024]{3,1,2,0:T(4,128)(2,1)S(1)} %slice_select_fusion.1), channel_id=1, source_target_pairs={{0,32},{32,0},{1,33},{33,1},{2,34},{34,2},{3,35},{35,3},{4,36},{36... | collective-permute-start | bytes 98312 | tf_op jit(solution)/shard_map/ppermute | solution.py:19
  39.1 112.1 %all-to-all-start.1 = ((bf16[192,64,128]{2,1,0:T(8,128)(2,1)}), bf16[192,64,128]{2,1,0:T(8,128)(2,1)}, u32[]{:S(2)}, u32[]{:S(2)}) async-start(bf16[192,64,128]{2,1,0:T(8,128)(2,1)} %gather_fusion.2), calls=%async_computation.1 | async-start | bytes 6291456 | tf_op jit(solution)/shard_map/all_to_all | solution.py:345
  46.6 13.0 %collective-permute-start.2 = (bf16[4,1,34,1024]{3,0,2,1:T(4,128)(2,1)S(1)}, bf16[4,1,34,1024]{3,0,2,1:T(4,128)(2,1)S(1)}, u32[]{:S(2)}, u32[]{:S(2)}) collective-permute-start(bf16[4,1,34,1024]{3,0,2,1:T(4,128)(2,1)S(1)} %copy.129), channel_id=1, source_target_pairs={{1,0},{2,1},{3,2},{4,3},{5,4},{6,5},{7,6},{8,7},{9,8},{10,9},{11,1... | collective-permute-start | bytes 835592 | tf_op jit(solution)/shard_map/ppermute | solution.py:31
  47.5 12.7 collective-permute-start.1
  62.7 62.0 %collective-permute-start.3 = (bf16[2,6,34,1024]{3,0,2,1:T(2,128)(2,1)S(1)}, bf16[2,6,34,1024]{3,0,2,1:T(2,128)(2,1)S(1)}, u32[]{:S(2)}, u32[]{:S(2)}) collective-permute-start(bf16[2,6,34,1024]{3,0,2,1:T(2,128)(2,1)S(1)} %copy.131), channel_id=1, source_target_pairs={{0,8},{1,9},{2,10},{3,11},{4,12},{5,13},{6,14},{7,15},{8,16},{9,17... | collective-permute-start | bytes 2506760 | tf_op jit(solution)/shard_map/ppermute | solution.py:41
  64.6 63.0 %copy-start.28 = (f32[1,1024]{1,0:T(1,128)}, f32[1,1024]{1,0:T(1,128)S(1)}, u32[]{:S(2)}) copy-start(f32[1,1024]{1,0:T(1,128)S(1)} %get-tuple-element.205) | copy-start | bytes 12292
  64.6 63.0 %copy-start.30 = (f32[1,1024]{1,0:T(1,128)}, f32[1,1024]{1,0:T(1,128)S(1)}, u32[]{:S(2)}) copy-start(f32[1,1024]{1,0:T(1,128)S(1)} %get-tuple-element.206) | copy-start | bytes 12292
  64.6 63.0 %copy-start.32 = (f32[1,1024]{1,0:T(1,128)}, f32[1,1024]{1,0:T(1,128)S(1)}, u32[]{:S(2)}) copy-start(f32[1,1024]{1,0:T(1,128)S(1)} %get-tuple-element.207) | copy-start | bytes 12292
  64.6 63.0 %copy-start.34 = (f32[1,1024]{1,0:T(1,128)}, f32[1,1024]{1,0:T(1,128)S(1)}, u32[]{:S(2)}) copy-start(f32[1,1024]{1,0:T(1,128)S(1)} %get-tuple-element.208) | copy-start | bytes 12292
  64.7 63.0 %copy-start.36 = (f32[1,1024]{1,0:T(1,128)}, f32[1,1024]{1,0:T(1,128)S(1)}, u32[]{:S(2)}) copy-start(f32[1,1024]{1,0:T(1,128)S(1)} %get-tuple-element.209) | copy-start | bytes 12292
  64.7 63.0 %copy-start.38 = (f32[1,1024]{1,0:T(1,128)}, f32[1,1024]{1,0:T(1,128)S(1)}, u32[]{:S(2)}) copy-start(f32[1,1024]{1,0:T(1,128)S(1)} %get-tuple-element.210) | copy-start | bytes 12292
  64.7 63.0 %copy-start.40 = (f32[1,1024]{1,0:T(1,128)}, f32[1,1024]{1,0:T(1,128)S(1)}, u32[]{:S(2)}) copy-start(f32[1,1024]{1,0:T(1,128)S(1)} %get-tuple-element.211) | copy-start | bytes 12292
  151.2 95.4 %all-to-all-start.2 = ((bf16[192,64,128]{2,1,0:T(8,128)(2,1)}), bf16[192,64,128]{2,1,0:T(8,128)(2,1)}, u32[]{:S(2)}, u32[]{:S(2)}) async-start(bf16[192,64,128]{2,1,0:T(8,128)(2,1)} %gather_fusion.3), calls=%async_computation.2 | async-start | bytes 6291456 | tf_op jit(solution)/shard_map/all_to_all | solution.py:346
  172.2 509.4 %all-gather.5.cloned.1.call-start = ((), (), s32[]{:S(2)}) async-start(), calls=%async_computation.6 | async-start | bytes 1064960 | tf_op jit(solution)/shard_map/all_gather | solution.py:305
  667.8 106.7 %all-to-all-start.4 = ((bf16[192,64,128]{2,1,0:T(8,128)(2,1)}), bf16[192,64,128]{2,1,0:T(8,128)(2,1)}, u32[]{:S(2)}, u32[]{:S(2)}) async-start(bf16[192,64,128]{2,1,0:T(8,128)(2,1)} %slice.690), calls=%async_computation.4 | async-start | bytes 6291456 | tf_op jit(solution)/shard_map/all_to_all | solution.py:377
  675.0 83.7 %all-gather.3.cloned.1.call-start = ((), (), s32[]{:S(2)}) async-start(), calls=%async_computation.5 | async-start | bytes 1064960 | tf_op jit(solution)/shard_map/all_gather | solution.py:306
  677.3 321.8 %all-reduce.6.cloned.1.call-start = ((), (), s32[]{:S(2)}) async-start(), calls=%async_computation.8 | async-start | bytes 8388608
  774.5 327.6 %all-to-all-start.3 = ((bf16[192,64,128]{2,1,0:T(8,128)(2,1)}), bf16[192,64,128]{2,1,0:T(8,128)(2,1)}, u32[]{:S(2)}, u32[]{:S(2)}) async-start(bf16[192,64,128]{2,1,0:T(8,128)(2,1)} %slice.691), calls=%async_computation.3 | async-start | bytes 6291456 | tf_op jit(solution)/shard_map/all_to_all | solution.py:370
  782.3 494.5 %all-reduce.4.cloned.1.call-start = ((), (), s32[]{:S(2)}) async-start(), calls=%async_computation.7 | async-start | bytes 262144 | tf_op jit(solution)/shard_map/psum | solution.py:413
  1055.2 17.4 %collective-permute-start.4 = (bf16[4,4,1,1024]{3,1,2,0:T(4,128)(2,1)S(1)}, bf16[4,4,1,1024]{3,1,2,0:T(4,128)(2,1)S(1)}, u32[]{:S(2)}, u32[]{:S(2)}) collective-permute-start(bf16[4,4,1,1024]{3,1,2,0:T(4,128)(2,1)S(1)} %fusion.112), channel_id=1, source_target_pairs={{0,32},{32,0},{1,33},{33,1},{2,34},{34,2},{3,35},{35,3},{4,36},{36... | collective-permute-start | bytes 98312 | tf_op jit(solution)/shard_map/ppermute | solution.py:19
  1073.5 14.2 %collective-permute-start.6 = (f32[4,1,34,1024]{3,1,2,0:T(1,128)S(1)}, f32[4,1,34,1024]{3,1,2,0:T(1,128)S(1)}, u32[]{:S(2)}, u32[]{:S(2)}) collective-permute-start(f32[4,1,34,1024]{3,1,2,0:T(1,128)S(1)} %get-tuple-element.180), channel_id=1, source_target_pairs={{0,1},{1,2},{2,3},{3,4},{4,5},{5,6},{6,7},{7,8},{8,9},{9,10},{10,1... | collective-permute-start | bytes 1671176 | tf_op jit(solution)/shard_map/ppermute | solution.py:29
  1075.4 12.7 collective-permute-start.5
  1091.3 43.7 %collective-permute-start.7 = (bf16[2,6,34,1024]{3,0,2,1:T(2,128)(2,1)}, bf16[2,6,34,1024]{3,0,2,1:T(2,128)(2,1)}, u32[]{:S(2)}, u32[]{:S(2)}) collective-permute-start(bf16[2,6,34,1024]{3,0,2,1:T(2,128)(2,1)} %copy.154), channel_id=1, source_target_pairs={{0,56},{1,57},{2,58},{3,59},{4,60},{5,61},{6,62},{7,63},{8,0},{9,1... | collective-permute-start | bytes 2506760 | tf_op jit(solution)/shard_map/ppermute | solution.py:41
  (130 other events, 1981.0 us)
Sparse Core Ops, SparseCore 0:
  175.7 79.8 all-gather.4
  679.1 79.5 all-gather.2
  769.3 229.8 all-reduce.5
  1102.2 174.5 all-reduce.3
where the time goes:
time: 1300 us; the launch traced here: 1290 us
  waiting for transfers between devices  513 us (39%)
  other arithmetic  365 us (28%)
  local copies, waits for them, and re-layouts  172 us (13%)
  matrix products  146 us (11%)
  starting transfers between devices  73.7 us (6%)
  between operations  16.7 us (1%)
    unnamed x5, waiting for transfers between devices  214 us
    psum x1, waiting for transfers between devices, shards(): filter_gradient = lax.psum(tap_grads, 'seq')  97.9 us
    scatter-add x8, other arithmetic, scan_step(): value_acc.at[flat_rows].add(value_grad)  83.1 us
    scatter-add x8, other arithmetic, scan_step(): key_acc.at[flat_rows].add(key_grad)  83 us
    all_gather x1, waiting for transfers between devices, shards(): lax.all_gather(averaged_value, 'seq', axis=0, tiled=True)  69.4 us
    all_to_all x1, waiting for transfers between devices, shards(): lax.all_to_all(own_values[asked_pairs], 'seq', split_axis=0, concat_axis=...  62.2 us
    ppermute x2, waiting for transfers between devices, passed_along(): return lax.ppermute(value, axis, pairs)  57.4 us
    convert_element_type x1, other arithmetic, shards(): value_gradient = from_lattice(value_lattice).astype(jnp.bfloat16)  36.2 us
  transfers between devices with their start and end apart: 17, of which 7 were waited for; matrix products, arithmetic and copies ran while one was open for 51% of the time, Pallas kernels for 0%

commit v1 on v0

v1 whole, which is shorter than its diff:
```python
import functools
import jax
import jax.numpy as jnp
from jax import lax
from jax.experimental import pallas as pl
from jax.experimental.pallas import tpu as pltpu
from jax.sharding import PartitionSpec as P

HEAD_DIM = 128
HEADS = 8
SLABS = 4
POOL = 12
BF = jnp.bfloat16
F32 = jnp.float32
TRAILER = 8
VMEM = pltpu.CompilerParams(vmem_limit_bytes=56 << 20)


def head_lanes(h):
    if isinstance(h, int):
        return slice(h * HEAD_DIM, (h + 1) * HEAD_DIM)
    return pl.ds(pl.multiple_of(h * HEAD_DIM, HEAD_DIM), HEAD_DIM)


def cube_rows(c):
    if isinstance(c, int):
        return slice(c * 64, c * 64 + 64)
    return pl.ds(pl.multiple_of(c * 64, 64), 64)


def mm(a, b, dims):
    return lax.dot_general(a, b, (dims, ((), ())), preferred_element_type=F32)


def whole(shape):
    zeros = (0,) * len(shape)
    return pl.BlockSpec(shape, lambda *_: zeros)


def gather_body(pairs, tokens, *rest, dests, slots):
    extra, out = rest if len(rest) == 2 else (None, rest[0])
    base = pl.program_id(0) * dests

    def one(d, carry):
        for s in range(slots):
            p = pairs[(base + d) * slots + s]
            out[d, cube_rows(s)] = tokens[cube_rows(p // HEADS), head_lanes(p % HEADS)]
        if extra is not None:
            out[d, slots * 64 :] = extra[d % HEADS]
        return carry

    lax.fori_loop(0, dests, one, 0, unroll=2)


def gather_pairs(pairs, tokens, devices, extra=None):
    slots = pairs.shape[0] // devices
    dests = devices // 4
    rows = slots * 64 + (0 if extra is None else extra.shape[1])
    operands = (tokens,) if extra is None else (tokens, extra)
    return pl.pallas_call(
        functools.partial(gather_body, dests=dests, slots=slots),
        grid_spec=pltpu.PrefetchScalarGridSpec(
            num_scalar_prefetch=1,
            grid=(4,),
            in_specs=[whole(x.shape) for x in operands],
            out_specs=pl.BlockSpec((dests, rows, HEAD_DIM), lambda i, *_: (i, 0, 0)),
        ),
        out_shape=jax.ShapeDtypeStruct((devices, rows, HEAD_DIM), tokens.dtype),
        compiler_params=VMEM,
        name="gather_pairs",
    )(pairs, *operands)


def fill_table(table, tokens, fetched, pairs, slots):
    for p in range(pairs):
        table[p] = tokens[cube_rows(p // HEADS), head_lanes(p % HEADS)]

    def one(d, carry):
        for s in range(slots):
            table[pairs + d * slots + s] = fetched[d, cube_rows(s)]
        return carry

    lax.fori_loop(0, fetched.shape[0], one, 0, unroll=2)


def clear(acc):
    def one(i, carry):
        acc[i] = jnp.zeros(acc.shape[1:], acc.dtype)
        return carry

    lax.fori_loop(0, acc.shape[0], one, 0, unroll=4)


def flush(acc, own, far, pairs, slots):
    def near(i, carry):
        own[i] = acc[i]
        return carry

    def distant(d, carry):
        for s in range(slots):
            far[d, cube_rows(s)] = acc[pairs + d * slots + s].astype(far.dtype)
        far[d, slots * 64 :] = jnp.zeros((far.shape[1] - slots * 64, HEAD_DIM), far.dtype)
        return carry

    lax.fori_loop(0, pairs, near, 0, unroll=4)
    lax.fori_loop(0, far.shape[0], distant, 0, unroll=2)


def picked(rows, cube, h):
    return [rows[(cube * HEADS + h) * 8 + i] for i in range(8)]


def probs_body(rows, query, grad, keys, far_keys, weights, own, far, table, acc, *, scale, pairs, slots):
    cube = pl.program_id(0)

    @pl.when(cube == 0)
    def _():
        fill_table(table, keys, far_keys, pairs, slots)
        clear(acc)

    def one_head(h):
        lanes = head_lanes(h)
        rs = picked(rows, cube, h)
        key_rows = jnp.concatenate([table[r] for r in rs], axis=0)
        logits = mm(query[:, lanes], key_rows, ((1,), (1,))) * scale
        expo = jnp.exp(logits - jnp.max(logits, axis=1, keepdims=True))
        w = expo / jnp.sum(expo, axis=1, keepdims=True)
        weights[h] = w
        part = mm(w.astype(BF), grad[:, lanes], ((0,), (0,)))
        for i, r in enumerate(rs):
            acc[r] += part[64 * i : 64 * i + 64]

    for h in range(HEADS):
        one_head(h)

    @pl.when(cube == pl.num_programs(0) - 1)
    def _():
        flush(acc, own, far, pairs, slots)


def fine_probs(rows, query, grad, keys, far_keys, slots, scale):
    cubes = query.shape[0] // 64
    pairs = cubes * HEADS
    devices = far_keys.shape[0]
    far_shape = (devices, slots * 64 + TRAILER, HEAD_DIM)
    width = HEADS * HEAD_DIM
    cube_block = pl.BlockSpec((64, width), lambda c, *_: (c, 0))
    return pl.pallas_call(
        functools.partial(probs_body, scale=scale, pairs=pairs, slots=slots),
        grid_spec=pltpu.PrefetchScalarGridSpec(
            num_scalar_prefetch=1,
            grid=(cubes,),
            in_specs=[cube_block, cube_block, whole(keys.shape), whole(far_keys.shape)],
            out_specs=[
                pl.BlockSpec((HEADS, 64, 512), lambda c, *_: (c, 0, 0)),
                whole((pairs, 64, HEAD_DIM)),
                whole(far_shape),
            ],
            scratch_shapes=[
                pltpu.VMEM((pairs + devices * slots, 64, HEAD_DIM), BF),
                pltpu.VMEM((pairs + devices * slots, 64, HEAD_DIM), F32),
            ],
        ),
        out_shape=[
            jax.ShapeDtypeStruct((pairs, 64, 512), F32),
            jax.ShapeDtypeStruct((pairs, 64, HEAD_DIM), F32),
            jax.ShapeDtypeStruct(far_shape, BF),
        ],
        compiler_params=VMEM,
        name="fine_probs",
    )(rows, query, grad, keys, far_keys)


def grads_body(
    rows, query, grad, keys, far_keys, values, far_values, weights,
    fine_out, fine_query, own, far, key_table, value_table, acc, *, scale, pairs, slots,
):
    cube = pl.program_id(0)

    @pl.when(cube == 0)
    def _():
        fill_table(key_table, keys, far_keys, pairs, slots)
        fill_table(value_table, values, far_values, pairs, slots)
        clear(acc)

    def one_head(h):
        lanes = head_lanes(h)
        rs = picked(rows, cube, h)
        key_rows = jnp.concatenate([key_table[r] for r in rs], axis=0)
        value_rows = jnp.concatenate([value_table[r] for r in rs], axis=0)
        g = grad[:, lanes]
        w = weights[h]
        out = mm(w.astype(BF), value_rows, ((1,), (0,)))
        delta = jnp.sum(g.astype(F32) * out, axis=1, keepdims=True)
        slope = mm(g, value_rows, ((1,), (1,)))
        ds = (w * (slope - delta)).astype(BF)
        fine_out[:, lanes] = out
        fine_query[:, lanes] = mm(ds, key_rows, ((1,), (0,))) * scale
        part = mm(ds, query[:, lanes], ((0,), (0,))) * scale
        for i, r in enumerate(rs):
            acc[r] += part[64 * i : 64 * i + 64]

    for h in range(HEADS):
        one_head(h)

    @pl.when(cube == pl.num_programs(0) - 1)
    def _():
        flush(acc, own, far, pairs, slots)


def fine_grads(rows, query, grad, keys, far_keys, values, far_values, weights, slots, scale):
    cubes = query.shape[0] // 64
    pairs = cubes * HEADS
    devices = far_keys.shape[0]
    far_shape = (devices, slots * 64 + TRAILER, HEAD_DIM)
    width = HEADS * HEAD_DIM
    cube_block = pl.BlockSpec((64, width), lambda c, *_: (c, 0))
    table = (pairs + devices * slots, 64, HEAD_DIM)
    return pl.pallas_call(
        functools.partial(grads_body, scale=scale, pairs=pairs, slots=slots),
        grid_spec=pltpu.PrefetchScalarGridSpec(
            num_scalar_prefetch=1,
            grid=(cubes,),
            in_specs=[
                cube_block,
                cube_block,
                whole(keys.shape),
                whole(far_keys.shape),
                whole(values.shape),
                whole(far_values.shape),
                pl.BlockSpec((HEADS, 64, 512), lambda c, *_: (c, 0, 0)),
            ],
            out_specs=[
                cube_block,
                cube_block,
                whole((pairs, 64, HEAD_DIM)),
                whole(far_shape),
            ],
            scratch_shapes=[
                pltpu.VMEM(table, BF),
                pltpu.VMEM(table, BF),
                pltpu.VMEM(table, F32),
            ],
        ),
        out_shape=[
            jax.ShapeDtypeStruct(query.shape, F32),
            jax.ShapeDtypeStruct(query.shape, F32),
            jax.ShapeDtypeStruct((pairs, 64, HEAD_DIM), F32),
            jax.ShapeDtypeStruct(far_shape, BF),
        ],
        compiler_params=VMEM,
        name="fine_grads",
    )(rows, query, grad, keys, far_keys, values, far_values, weights)


def collect_body(pairs, own, back, share, out, acc):
    for p in range(own.shape[0]):
        c, h = p // HEADS, p % HEADS
        acc[cube_rows(c), head_lanes(h)] = own[p] + share[c : c + 1, head_lanes(h)] * (1.0 / 64.0)

    slots = pairs.shape[0] // back.shape[0]

    def one(d, carry):
        for s in range(slots):
            p = pairs[d * slots + s]
            rows = cube_rows(p // HEADS)
            lanes = head_lanes(p % HEADS)
            acc[rows, lanes] += back[d, cube_rows(s)].astype(F32)
        return carry

    lax.fori_loop(0, back.shape[0], one, 0)
    out[...] = acc[...].astype(out.dtype)


def collect(pairs, own, back, share, dtype):
    shape = (own.shape[0] // HEADS * 64, HEADS * HEAD_DIM)
    return pl.pallas_call(
        collect_body,
        grid_spec=pltpu.PrefetchScalarGridSpec(
            num_scalar_prefetch=1,
            grid=(1,),
            in_specs=[whole(own.shape), whole(back.shape), whole(share.shape)],
            out_specs=whole(shape),
            scratch_shapes=[pltpu.VMEM(shape, F32)],
        ),
        out_shape=jax.ShapeDtypeStruct(shape, dtype),
        compiler_params=VMEM,
        name="collect",
    )(pairs, own, back, share)


def put_halves(target, sem, stage, parts):
    for i, part in enumerate(parts):
        high = part.astype(BF)
        stage[:, i] = high
        stage[:, len(parts) + i] = (part - high.astype(F32)).astype(BF)
    rows = target.shape[1]
    copy = pltpu.make_async_copy(
        stage, target.at[:, pl.ds(rows - TRAILER, TRAILER)], sem
    )
    copy.start()
    copy.wait()


def from_halves(received):
    halves = received[:, -TRAILER:].astype(F32)
    return halves[:, : TRAILER // 2] + halves[:, TRAILER // 2 :]


def coarse_body(block, query, key, grad, value, back, out, stage, sem, *, scale):
    del back
    q, k, g, v = query[...], key[...], grad[...], value[...]
    logits = mm(k, q, ((1,), (1,))) * scale
    expo = jnp.exp(logits - jnp.max(logits, axis=0, keepdims=True))
    w = expo / jnp.sum(expo, axis=0, keepdims=True)
    wr = w.astype(BF)
    slope = mm(v, g, ((1,), (1,)))
    delta = jnp.sum(wr.astype(F32) * slope, axis=0, keepdims=True)
    ds = (w * (slope - delta)).astype(BF)
    results = (
        mm(wr, v, ((0,), (0,))),
        mm(ds, k, ((0,), (0,))) * scale,
        mm(ds, q, ((1,), (0,))) * scale,
        mm(wr, g, ((1,), (0,))),
    )
    shape = (results[0].shape[0] // 8, 8, HEAD_DIM)
    mine = lax.broadcasted_iota(jnp.int32, shape, 1) == block[0]
    parts = [jnp.sum(jnp.where(mine, r.reshape(shape), 0.0), axis=1) for r in results]
    put_halves(out, sem, stage, parts)


def coarse_head(block, pooled, back, scale):
    anywhere = pl.BlockSpec(memory_space=pl.ANY)
    return pl.pallas_call(
        functools.partial(coarse_body, scale=scale),
        grid_spec=pltpu.PrefetchScalarGridSpec(
            num_scalar_prefetch=1,
            grid=(1,),
            in_specs=[whole(x.shape) for x in pooled] + [anywhere],
            out_specs=anywhere,
            scratch_shapes=[
                pltpu.VMEM((back.shape[0], TRAILER, HEAD_DIM), BF),
                pltpu.SemaphoreType.DMA,
            ],
        ),
        out_shape=jax.ShapeDtypeStruct(back.shape, back.dtype),
        input_output_aliases={5: 0},
        compiler_params=VMEM,
        name="coarse_head",
    )(block, *pooled, back)


def taps_body(grad, framed, out, wide):
    frames, height, breadth = grad.shape[:3]
    planes, rows = framed.shape[:2]
    for t in range(planes):
        for r in range(rows):
            wide[t * rows + r, 0 : framed.shape[2]] = framed[t, r].astype(F32)
    for col in range(3):
        sums = {}
        for t in range(planes):
            for r in range(rows):
                cells = wide[t * rows + r, col : col + breadth]
                for back in range(3):
                    for row in range(3):
                        f, y = t - 2 + back, r - row
                        if 0 <= f < frames and 0 <= y < height:
                            tap = 9 * back + 3 * row + col
                            term = jnp.sum((grad[f, y] * cells).reshape(-1, 8, 128), axis=0)
                            sums[tap] = sums[tap] + term if tap in sums else term
        for tap, total in sums.items():
            out[tap : tap + 1] = jnp.sum(total, axis=0, keepdims=True)
    out[27:] = jnp.zeros((out.shape[0] - 27, 128), F32)


def tap_gradients(grad, framed):
    width = grad.shape[3]
    return pl.pallas_call(
        taps_body,
        grid=(width // 128,),
        in_specs=[
            pl.BlockSpec(grad.shape[:3] + (128,), lambda i: (0, 0, 0, i)),
            pl.BlockSpec(framed.shape[:3] + (128,), lambda i: (0, 0, 0, i)),
        ],
        out_specs=pl.BlockSpec((32, 128), lambda i: (0, i)),
        scratch_shapes=[pltpu.VMEM((framed.shape[0] * framed.shape[1], 40, 128), F32)],
        out_shape=jax.ShapeDtypeStruct((32, width), F32),
        compiler_params=VMEM,
        name="tap_gradients",
    )(grad, framed)


def sum_body(shares, back, out, stage, sem):
    del back
    total = shares[0]
    for d in range(1, shares.shape[0]):
        total = total + shares[d]
    for i in range(TRAILER // 2):
        high = total[i : i + 1].astype(BF)
        low = (total[i : i + 1] - high.astype(F32)).astype(BF)
        for half, row in ((0, high), (TRAILER // 2, low)):
            stage[:, half + i] = jnp.broadcast_to(row, (stage.shape[0], HEAD_DIM))
    copy = pltpu.make_async_copy(
        stage, out.at[:, pl.ds(out.shape[1] - TRAILER, TRAILER)], sem
    )
    copy.start()
    copy.wait()


def sum_taps(shares, back):
    anywhere = pl.BlockSpec(memory_space=pl.ANY)
    return pl.pallas_call(
        sum_body,
        in_specs=[pl.BlockSpec(memory_space=pltpu.VMEM), anywhere],
        out_specs=anywhere,
        scratch_shapes=[
            pltpu.VMEM((back.shape[0], TRAILER, HEAD_DIM), BF),
            pltpu.SemaphoreType.DMA,
        ],
        out_shape=jax.ShapeDtypeStruct(back.shape, back.dtype),
        input_output_aliases={1: 0},
        compiler_params=VMEM,
        name="sum_taps",
    )(shares, back)


def from_partner(block, axis, apart):
    count = lax.axis_size(axis)
    route = []
    for low in range(count):
        high = low | 1 << apart
        if high != low and high < count:
            route += [(low, high), (high, low)]
    return lax.ppermute(block, axis, route)


def with_halo(cells, sides, width):
    for axis, dim in sides:
        count = lax.axis_size(axis)
        head = lax.slice_in_dim(cells, 0, width, axis=dim)
        tail = lax.slice_in_dim(cells, cells.shape[dim] - width, cells.shape[dim], axis=dim)
        cells = jnp.concatenate(
            [
                lax.ppermute(tail, axis, [(i, (i + 1) % count) for i in range(count)]),
                cells,
                lax.ppermute(head, axis, [((i + 1) % count, i) for i in range(count)]),
            ],
            axis=dim,
        )
    return cells


def passed_along(value, axis, steps):
    count = lax.axis_size(axis)
    pairs = [(source, (source + steps) % count) for source in range(count)]
    return lax.ppermute(value, axis, pairs)


def to_lattice(tokens):
    channels = tokens.shape[1]
    cube_count = tokens.shape[0] // 64
    lattice = tokens.reshape(cube_count, 4, 4, 4, channels).transpose(1, 2, 0, 3, 4)
    return lattice.reshape(4, 4, cube_count * 4, channels)


def from_lattice(lattice):
    channels = lattice.shape[3]
    cube_count = lattice.shape[2] // 4
    tokens = lattice.reshape(4, 4, cube_count, 4, channels).transpose(2, 0, 1, 3, 4)
    return tokens.reshape(cube_count * 64, channels)


def side_columns(lattice, edge, col_half):
    blank = jnp.zeros_like(edge)
    return jnp.concatenate(
        [jnp.where(col_half == 1, edge, blank), lattice, jnp.where(col_half == 0, edge, blank)],
        axis=2,
    )


def clear_rims(extended, row_band, band_count):
    blank = jnp.zeros_like(extended[:, :1])
    upper = jnp.where(row_band > 0, extended[:, :1], blank)
    lower = jnp.where(row_band < band_count - 1, extended[:, -1:], blank)
    return jnp.concatenate([upper, extended[:, 1:-1], lower], axis=1)


def convolve_values(framed, filter_taps):
    frames = framed.shape[0] - 2
    height = framed.shape[1] - 2
    breadth = framed.shape[2] - 2
    totaled_sum = jnp.zeros((frames, height, breadth, framed.shape[3]), jnp.float32)
    for back_step in range(3):
        for row_step in (-1, 0, 1):
            for col_step in (-1, 0, 1):
                tap_index = back_step * 9 + (row_step + 1) * 3 + col_step + 1
                shifted = framed[
                    2 - back_step : 2 - back_step + frames,
                    1 + row_step : 1 + row_step + height,
                    1 + col_step : 1 + col_step + breadth,
                ]
                totaled_sum = totaled_sum + filter_taps[tap_index] * shifted.astype(jnp.float32)
    return totaled_sum


def convolve_back(grad_space, filter_taps):
    frames = grad_space.shape[0] - 2
    height = grad_space.shape[1] - 2
    breadth = grad_space.shape[2] - 2
    total = jnp.zeros((frames, height, breadth, grad_space.shape[3]), F32)
    for back_step in range(3):
        for row_step in (-1, 0, 1):
            for col_step in (-1, 0, 1):
                tap_index = back_step * 9 + (row_step + 1) * 3 + col_step + 1
                total = total + filter_taps[tap_index] * grad_space[
                    back_step : back_step + frames,
                    1 - row_step : 1 - row_step + height,
                    1 - col_step : 1 - col_step + breadth,
                ]
    return total


def pool_cubes(tokens):
    return jnp.mean(
        tokens.astype(jnp.float32).reshape(tokens.shape[0] // 64, 64, tokens.shape[1]), axis=1
    )


def spread(per_cube):
    cube_count = per_cube.shape[0]
    return jnp.broadcast_to(per_cube[:, None, :], (cube_count, 64, per_cube.shape[1])).reshape(
        cube_count * 64, per_cube.shape[1]
    )


def exchanged(rows):
    return lax.all_to_all(rows, "seq", split_axis=0, concat_axis=0, tiled=True)


def after(value, *earlier):
    return lax.optimization_barrier((value, *earlier))[0]


def shards(query_tokens, key_tokens, value_tokens, gate_tokens, filter_taps, selected, cotangent):
    devices = lax.axis_size("seq")
    device_index = lax.axis_index("seq")
    cube_count = query_tokens.shape[0] // 64
    pair_count = cube_count * HEADS
    channels = HEADS * HEAD_DIM
    capacity = max(3, 2 * HEADS * POOL // (devices - 1))
    logit_scale = HEAD_DIM ** (-0.5)
    band_count = devices // (2 * SLABS)
    rotated = (device_index + 2 * band_count + band_count // 2) % devices
    row_band = rotated % band_count
    slab_index = rotated // band_count % SLABS
    col_half = rotated // (devices // 2)
    col_bit = devices.bit_length() - 2

    owner_device = selected // cube_count
    pair_index = selected % cube_count * HEADS + jnp.arange(HEADS, dtype=jnp.int32)[None, :, None]
    remote_flat = (owner_device != device_index).reshape(-1)
    pair_codes = (owner_device * pair_count + pair_index).reshape(-1)
    matches = (
        pair_codes[:, None] == jnp.arange(devices * pair_count, dtype=jnp.int32)[None, :]
    ) & remote_flat[:, None]
    present = jnp.any(matches, axis=0).reshape(devices, pair_count).astype(jnp.int32)
    slot_rank = jnp.cumsum(present, axis=1) - present
    in_slot = (slot_rank[:, :, None] == jnp.arange(capacity, dtype=jnp.int32)[None, None, :]) & (
        present[:, :, None] > 0
    )
    requests = jnp.sum(
        in_slot.astype(jnp.int32) * jnp.arange(pair_count, dtype=jnp.int32)[None, :, None], axis=1
    ).reshape(-1)
    asked_pairs = exchanged(requests)
    slot_of = jnp.sum(matches.astype(jnp.int32) * slot_rank.reshape(-1)[None, :], axis=1)
    table_row = jnp.where(
        remote_flat,
        pair_count + owner_device.reshape(-1) * capacity + slot_of,
        pair_index.reshape(-1),
    )

    lattice = to_lattice(value_tokens)
    value_edge = from_partner(
        jnp.where(col_half == 0, lattice[:, :, -1:], lattice[:, :, :1]), "seq", col_bit
    )
    value_wide = side_columns(lattice, value_edge, col_half)
    value_tall = clear_rims(with_halo(value_wide, (("seq", 1),), 1), row_band, band_count)
    prior_frames = passed_along(value_tall[-2:], "seq", band_count)
    prior_frames = jnp.where(slab_index > 0, prior_frames, jnp.zeros_like(prior_frames))
    framed = jnp.concatenate([prior_frames, value_tall], axis=0)

    far_keys = exchanged(after(gather_pairs(asked_pairs, key_tokens, devices), framed))

    filtered = from_lattice(convolve_values(framed, filter_taps)).astype(BF)
    gated = cotangent.astype(F32) * gate_tokens.astype(F32)
    pooled = jnp.stack(
        [
            pool_cubes(query_tokens).astype(BF),
            pool_cubes(key_tokens).astype(BF),
            jnp.sum(gated.reshape(cube_count, 64, channels), axis=1).astype(BF),
            pool_cubes(filtered).astype(BF),
        ],
        axis=1,
    )
    pooled = pooled.reshape(cube_count, 4, HEADS, HEAD_DIM).transpose(2, 1, 0, 3)
    pooled = pooled.reshape(HEADS, 4 * cube_count, HEAD_DIM)
    far_values = exchanged(after(gather_pairs(asked_pairs, filtered, devices, pooled), far_keys))
    one_head = far_values[:, capacity * 64 :].reshape(devices, 4, cube_count, HEAD_DIM)
    one_head = one_head.transpose(1, 0, 2, 3).reshape(4, devices * cube_count, HEAD_DIM)

    weights, own_value, back_value = fine_probs(
        table_row, query_tokens, cotangent, key_tokens, far_keys, capacity, logit_scale
    )
    block = (device_index // HEADS).reshape(1)
    back_value = exchanged(coarse_head(block, tuple(one_head), back_value, logit_scale))
    fine_out, fine_query, own_key, back_key = fine_grads(
        table_row, query_tokens, cotangent, key_tokens, far_keys, filtered, far_values, weights,
        capacity, logit_scale,
    )
    coarse = from_halves(back_value).reshape(cube_count, HEADS, 4, HEAD_DIM)
    coarse = coarse.transpose(2, 0, 1, 3).reshape(4, cube_count, channels)
    coarse_out, coarse_query, coarse_key, coarse_value = coarse

    coarse_tokens = spread(coarse_out)
    attended = (fine_out + gate_tokens.astype(F32) * coarse_tokens).astype(BF)
    gate_gradient = (cotangent.astype(F32) * coarse_tokens).astype(BF)
    query_gradient = (fine_query + spread(coarse_query) / 64.0).astype(BF)

    filtered_grad = collect(
        asked_pairs, after(own_value, back_key), back_value, coarse_value, F32
    )
    grad_lattice = to_lattice(filtered_grad)
    grad_edge = from_partner(
        jnp.where(col_half == 0, grad_lattice[:, :, -1:], grad_lattice[:, :, :1]).astype(BF),
        "seq",
        col_bit,
    ).astype(F32)
    grad_wide = side_columns(grad_lattice, grad_edge, col_half)
    grad_tall = clear_rims(with_halo(grad_wide, (("seq", 1),), 1), row_band, band_count)
    next_frames = passed_along(grad_tall[:2].astype(BF), "seq", -band_count).astype(F32)
    next_frames = jnp.where(slab_index < SLABS - 1, next_frames, jnp.zeros_like(next_frames))
    grad_space = jnp.concatenate([grad_tall, next_frames], axis=0)
    shares = exchanged(tap_gradients(grad_lattice, framed).reshape(devices, TRAILER // 2, HEAD_DIM))
    back_key = exchanged(after(sum_taps(shares, back_key), grad_space))
    filter_gradient = from_halves(back_key).reshape(-1, channels)[: filter_taps.shape[0]]
    value_gradient = from_lattice(convolve_back(grad_space, filter_taps)).astype(BF)
    key_gradient = collect(asked_pairs, own_key, back_key, coarse_key, BF)
    return (attended, query_gradient, key_gradient, value_gradient, gate_gradient, filter_gradient)


def solution(mesh):
    return jax.shard_map(
        shards,
        mesh=mesh,
        in_specs=(
            P(("dp", "seq"), None),
            P(("dp", "seq"), None),
            P(("dp", "seq"), None),
            P(("dp", "seq"), None),
            P(),
            P(("dp", "seq"), None, None),
            P(("dp", "seq"), None),
        ),
        out_specs=(
            P(("dp", "seq"), None),
            P(("dp", "seq"), None),
            P(("dp", "seq"), None),
            P(("dp", "seq"), None),
            P(("dp", "seq"), None),
            P("dp", None),
        ),
        check_vma=False,
    )
```

time: 1300 us -> 494 us (0.38)
  other arithmetic: 365 us -> 48.6 us
  waiting for transfers between devices: 513 us -> 254 us
  matrix products: 146 us -> 0 us
  local copies, waits for them, and re-layouts: 172 us -> 26.9 us
  Pallas kernels: 0 us -> 86.5 us
  between operations: 16.7 us -> 2.68 us
    scatter-add x18 -> x0, other arithmetic: 216 us -> none  [the longest x8 83.1 us: scan_step(): value_acc.at[flat_rows].add(value_grad)]
    unnamed x5 -> x0, waiting for transfers between devices: 214 us -> none
    all_to_all x5 -> x6, waiting for transfers between devices: 63.4 us -> 232 us  [exchanged(): return lax.all_to_all(rows, 'seq', split_axis=0, concat_axis=0, tiled=True)]
    dot_general x54 -> x0, matrix products: 146 us -> none  [the longest x8 34.8 us: attend_cube(): jnp.einsum('hqk,hqd->hkd', rounded_result, grad_cube, preferred_element_t...]
    psum x1 -> x0, waiting for transfers between devices: 97.9 us -> none  [shards(): filter_gradient = lax.psum(tap_grads, 'seq')]
    pallas_call x0 -> x9, Pallas kernels: none -> 86.5 us  [the longest x1 28.4 us: fine_grads(): pl.pallas_call(functools.partial(grads_body, scale=scale, pairs=pairs, sl...]
    all_gather x2 -> x0, waiting for transfers between devices: 69.4 us -> none  [the longest x1 69.4 us: shards(): lax.all_gather(averaged_value, 'seq', axis=0, tiled=True)]
    gather x18 -> x0, local copies, waits for them, and re-layouts: 68.1 us -> none  [the longest x8 30.7 us: attend_cube(): table_key[flat_rows].reshape(head_count, pick_count * 64, HEAD_DIM)]
  transfers between devices with their start and end apart: 17 -> 14, of which waited for: 7 -> 12; matrix products, arithmetic and copies ran while one was open for 51% -> 10% of each run, Pallas kernels for 0% -> 14%
where the time goes in v1:
time: 494 us; the launch traced here: 485 us
  waiting for transfers between devices  254 us (51%)
  Pallas kernels  86.5 us (18%)
  starting transfers between devices  65.9 us (13%)
  other arithmetic  48.6 us (10%)
  local copies, waits for them, and re-layouts  26.9 us (5%)
    all_to_all x6, waiting for transfers between devices, exchanged(): return lax.all_to_all(rows, 'seq', split_axis=0, concat_axis=0, tiled=True)  232 us
    all_to_all x6, starting transfers between devices, exchanged(): return lax.all_to_all(rows, 'seq', split_axis=0, concat_axis=0, tiled=True)  46.3 us
    pallas_call x1, Pallas kernels, fine_grads(): pl.pallas_call(functools.partial(grads_body, scale=scale, pairs=pairs, sl...  28.4 us
    pallas_call x1, Pallas kernels, fine_probs(): pl.pallas_call(functools.partial(probs_body, scale=scale, pairs=pairs, sl...  21.1 us
    pallas_call x2, Pallas kernels, collect(): pl.pallas_call(collect_body, grid_spec=pltpu.PrefetchScalarGridSpec(num_s...  13.7 us
    reduce_sum x4, other arithmetic, pool_cubes(): jnp.mean(tokens.astype(jnp.float32).reshape(tokens.shape[0] // 64, 64, to...  12.3 us
    pallas_call x2, Pallas kernels, gather_pairs(): pl.pallas_call(functools.partial(gather_body, dests=dests, slots=slots),...  10.3 us
    ppermute x2, starting transfers between devices, from_partner(): return lax.ppermute(block, axis, route)  10.2 us
  transfers between devices with their start and end apart: 14, of which 12 were waited for; matrix products, arithmetic and copies ran while one was open for 10% of the time, Pallas kernels for 14%

profile of v1, /device:TPU:1, one launch (start us, length us, event | category | flops | bytes accessed | tf_op | source)
XLA Modules:
  0.0 484.9 jit_solution(7226658556774383345)
XLA Ops:
  3.1 7.8 %collective-permute-start = (bf16[4,4,1,1024]{3,2,1,0:T(2,128)(2,1)S(1)}, bf16[4,4,1,1024]{3,2,1,0:T(2,128)(2,1)S(1)}, u32[]{:S(2)}, u32[]{:S(2)}) collective-permute-start(bf16[4,4,1,1024]{3,2,1,0:T(2,128)(2,1)S(1)} %broadcast_select_fusion.5), channel_id=1, source_target_pairs={{0,32},{32,0},{1,33},{33,1},{2,34},{34,2},{3,35},{35,3},{4,36},{36... | collective-permute-start | bytes 98312 | tf_op jit(solution)/shard_map/ppermute | solution.py:434
  30.7 11.3 %all-to-all-start = ((s32[64,3,1]{1,2,0:T(1,128)}), s32[64,3,1]{1,2,0:T(1,128)S(1)}, u32[]{:S(2)}, u32[]{:S(2)}) async-start(s32[64,3,1]{1,2,0:T(1,128)} %copy.59), calls=%async_computation | async-start | bytes 65536 | tf_op jit(solution)/shard_map/all_to_all | solution.py:537
  42.1 11.3 %all-to-all-done = s32[64,3,1]{1,2,0:T(1,128)S(1)} async-done(((s32[64,3,1]{1,2,0:T(1,128)}), s32[64,3,1]{1,2,0:T(1,128)S(1)}, u32[]{:S(2)}, u32[]{:S(2)}) %all-to-all-start) | async-done | bytes 800 | tf_op jit(solution)/shard_map/all_to_all | solution.py:537
  55.3 5.1 %gather_pairs.2 = bf16[64,192,128]{2,1,0:T(8,128)(2,1)} custom-call(s32[192]{0:T(256)} %all_to_all.24.pairs, bf16[512,1024]{1,0:T(8,128)(2,1)} %keys.3), custom_call_target="tpu_custom_call" | custom-call | tf_op jit(solution)/shard_map/gather_pairs/pallas_call | solution.py:60
  61.8 6.0 %all-to-all-start.1 = ((bf16[64,192,128]{2,1,0:T(8,128)(2,1)}), bf16[64,192,128]{2,1,0:T(8,128)(2,1)}, u32[]{:S(2)}, u32[]{:S(2)}) async-start(bf16[64,192,128]{2,1,0:T(8,128)(2,1)} %gather_pairs.2), calls=%async_computation.1 | async-start | bytes 6291456 | tf_op jit(solution)/shard_map/all_to_all | solution.py:537
  74.7 9.2 %convert_reduce_fusion.2 = (f32[32,1024]{1,0:T(8,128)S(1)}, bf16[4,4,32,1024]{3,2,1,0:T(8,128)(2,1)}) fusion(bf16[6,6,34,1024]{3,2,1,0:T(8,128)(2,1)S(1)} %maximum_maximum_fusion.1.framed, f32[1024]{0:T(1024)S(1)} %bitcast.128, f32[1024]{0:T(1024)S(1)} %bitcast.130, f32[1024]{0:T(1024)S(1)} %bitcast.134, f32[1024]{0:T(1024)S(1)} %bitcast.136, ...), kind=kLoop, calls=%fused_computation.75 | loop fusion | flops 46628864 | bytes 27570176 | tf_op jit(solution)/shard_map/reduce_sum | solution.py:524
  87.8 5.2 %gather_pairs.3 = bf16[64,224,128]{2,1,0:T(8,128)(2,1)} custom-call(s32[192]{0:T(256)} %all_to_all.24.pairs, bf16[512,1024]{1,0:T(8,128)(2,1)} %convert_element_type.254.tokens.values, bf16[8,32,128]{2,1,0:T(8,128)(2,1)} %maximum_bitcast_fusion.rest_0_), custom_call_target="tpu_custom_call" | custom-call | tf_op jit(solution)/shard_map/gather_pairs/pallas_call | solution.py:60
  93.0 47.3 %all-to-all-done.1.far_keys = bf16[64,192,128]{2,1,0:T(8,128)(2,1)} async-done(((bf16[64,192,128]{2,1,0:T(8,128)(2,1)}), bf16[64,192,128]{2,1,0:T(8,128)(2,1)}, u32[]{:S(2)}, u32[]{:S(2)}) %all-to-all-start.1) | async-done | bytes 3145760 | tf_op jit(solution)/shard_map/all_to_all | solution.py:537
  140.3 6.7 %all-to-all-start.2 = ((bf16[64,224,128]{2,1,0:T(8,128)(2,1)}), bf16[64,224,128]{2,1,0:T(8,128)(2,1)}, u32[]{:S(2)}, u32[]{:S(2)}) async-start(bf16[64,224,128]{2,1,0:T(8,128)(2,1)} %gather_pairs.3), calls=%async_computation.2 | async-start | bytes 7340032 | tf_op jit(solution)/shard_map/all_to_all | solution.py:537
  150.2 21.1 %fine_probs.1 = (f32[64,64,512]{2,1,0:T(8,128)}, f32[64,64,128]{2,1,0:T(8,128)}, bf16[64,200,128]{2,1,0:T(8,128)(2,1)}) custom-call(s32[512]{0:T(512)} %add_select_fusion.2.rows, bf16[512,1024]{1,0:T(8,128)(2,1)} %query.3, bf16[512,1024]{1,0:T(8,128)(2,1)} %grad.3, bf16[512,1024]{1,0:T(8,128)(2,1)} %keys.3, bf16[64,192,128]{2,1,0:T(8,128)(2,1)} %all-to-all-done.1.far_keys), custom_call_target="tpu_custom_call" | custom-call | tf_op jit(solution)/shard_map/fine_probs/pallas_call | solution.py:148
  171.3 59.4 %all-to-all-done.2.far_values = bf16[64,224,128]{2,1,0:T(8,128)(2,1)} async-done(((bf16[64,224,128]{2,1,0:T(8,128)(2,1)}), bf16[64,224,128]{2,1,0:T(8,128)(2,1)}, u32[]{:S(2)}, u32[]{:S(2)}) %all-to-all-start.2) | async-done | bytes 3670048 | tf_op jit(solution)/shard_map/all_to_all | solution.py:537
  236.0 7.0 %all-to-all-start.3 = ((bf16[64,200,128]{2,1,0:T(8,128)(2,1)}), bf16[64,200,128]{2,1,0:T(8,128)(2,1)S(1)}, u32[]{:S(2)}, u32[]{:S(2)}) async-start(bf16[64,200,128]{2,1,0:T(8,128)(2,1)} %coarse_head.1), calls=%async_computation.3 | async-start | bytes 6553600 | tf_op jit(solution)/shard_map/all_to_all | solution.py:537
  243.0 28.4 %fine_grads.1 = (f32[512,1024]{1,0:T(8,128)}, f32[512,1024]{1,0:T(8,128)}, f32[64,64,128]{2,1,0:T(8,128)}, bf16[64,200,128]{2,1,0:T(8,128)(2,1)}) custom-call(s32[512]{0:T(512)} %add_select_fusion.2.rows, bf16[512,1024]{1,0:T(8,128)(2,1)} %query.3, bf16[512,1024]{1,0:T(8,128)(2,1)} %grad.3, bf16[512,1024]{1,0:T(8,128)(2,1)} %keys.3, ...), custom_call_target="tpu_custom_call" | custom-call | tf_op jit(solution)/shard_map/fine_grads/pallas_call | solution.py:219
  271.5 46.6 %all-to-all-done.3.back = bf16[64,200,128]{2,1,0:T(8,128)(2,1)S(1)} async-done(((bf16[64,200,128]{2,1,0:T(8,128)(2,1)}), bf16[64,200,128]{2,1,0:T(8,128)(2,1)S(1)}, u32[]{:S(2)}, u32[]{:S(2)}) %all-to-all-start.3) | async-done | bytes 3276832 | tf_op jit(solution)/shard_map/all_to_all | solution.py:537
  319.9 7.0 %collect.2 = f32[512,1024]{1,0:T(8,128)} custom-call(s32[192]{0:T(256)} %all_to_all.24.pairs, f32[64,64,128]{2,1,0:T(8,128)} %get-tuple-element.26.own, bf16[64,200,128]{2,1,0:T(8,128)(2,1)} %copy-done.8, f32[8,1024]{1,0:T(8,128)} %get-tuple-element.45.share), custom_call_target="tpu_custom_call" | custom-call | tf_op jit(solution)/shard_map/collect/pallas_call | solution.py:277
  340.4 4.9 %collective-permute-start.5 = (f32[4,1,34,1024]{3,0,2,1:T(4,128)S(1)}, f32[4,1,34,1024]{3,0,2,1:T(4,128)S(1)}, u32[]{:S(2)}, u32[]{:S(2)}) collective-permute-start(f32[4,1,34,1024]{3,0,2,1:T(4,128)S(1)} %copy.71), channel_id=1, source_target_pairs={{0,1},{1,2},{2,3},{3,4},{4,5},{5,6},{6,7},{7,8},{8,9},{9,10},{10,1... | collective-permute-start | bytes 1671176 | tf_op jit(solution)/shard_map/ppermute | solution.py:444
  345.8 6.0 %collective-permute-done.5 = f32[4,1,34,1024]{3,0,2,1:T(4,128)S(1)} collective-permute-done((f32[4,1,34,1024]{3,0,2,1:T(4,128)S(1)}, f32[4,1,34,1024]{3,0,2,1:T(4,128)S(1)}, u32[]{:S(2)}, u32[]{:S(2)}) %collective-permute-start.5) | collective-permute-done | bytes 557088 | tf_op jit(solution)/shard_map/ppermute | solution.py:444
  357.5 7.7 %tap_gradients.1 = f32[32,1024]{1,0:T(8,128)} custom-call(f32[4,4,32,1024]{3,2,1,0:T(8,128)} %copy-done.1, bf16[6,6,34,1024]{3,2,1,0:T(8,128)(2,1)} %copy-done), custom_call_target="tpu_custom_call" | custom-call | tf_op jit(solution)/shard_map/tap_gradients/pallas_call | solution.py:378
  366.8 9.7 %all-to-all-start.4 = ((f32[64,4,128]{2,1,0:T(4,128)}), f32[64,4,128]{2,1,0:T(4,128)S(1)}, u32[]{:S(2)}, u32[]{:S(2)}) async-start(f32[64,4,128]{2,1,0:T(4,128)} %reshape.249), calls=%async_computation.4 | async-start | bytes 262144 | tf_op jit(solution)/shard_map/all_to_all | solution.py:537
  376.5 11.1 %all-to-all-done.4.shares = f32[64,4,128]{2,1,0:T(4,128)S(1)} async-done(((f32[64,4,128]{2,1,0:T(4,128)}), f32[64,4,128]{2,1,0:T(4,128)S(1)}, u32[]{:S(2)}, u32[]{:S(2)}) %all-to-all-start.4) | async-done | bytes 131104 | tf_op jit(solution)/shard_map/all_to_all | solution.py:537
  395.0 5.6 %all-to-all-start.5 = ((bf16[64,200,128]{2,1,0:T(8,128)(2,1)}), bf16[64,200,128]{2,1,0:T(8,128)(2,1)}, u32[]{:S(2)}, u32[]{:S(2)}) async-start(bf16[64,200,128]{2,1,0:T(8,128)(2,1)} %sum_taps.1), calls=%async_computation.5 | async-start | bytes 6553600 | tf_op jit(solution)/shard_map/all_to_all | solution.py:537
  409.2 8.4 %fusion.6 = bf16[4,4,32,1024]{3,2,1,0:T(8,128)(2,1)S(1)} fusion(f32[6,6,34,1024]{3,2,1,0:T(8,128)S(1)} %bitcast.108, f32[4,5,34,1024]{3,2,1,0:T(8,128)S(1)} %get-tuple-element.31, f32[4,4,32,1024]{3,2,1,0:T(8,128)S(1)} %copy-done.2, f32[4,4,1,1024]{3,2,1,0:T(1,128)S(1)} %get-tuple-element.75, f32[4,4,1,1024]{3,2,1,0:T(1,128)S(1)} %get-tuple-element.76, ...), kind=kLoop, calls=%fused_computation.16 | loop fusion | flops 29360128 | bytes 53719040 | tf_op jit(solution)/shard_map/convert_element_type | solution.py:646
  419.7 56.4 %all-to-all-done.5.back = bf16[64,200,128]{2,1,0:T(8,128)(2,1)} async-done(((bf16[64,200,128]{2,1,0:T(8,128)(2,1)}), bf16[64,200,128]{2,1,0:T(8,128)(2,1)}, u32[]{:S(2)}, u32[]{:S(2)}) %all-to-all-start.5) | async-done | bytes 3276832 | tf_op jit(solution)/shard_map/all_to_all | solution.py:537
  477.8 6.6 %collect.3 = bf16[512,1024]{1,0:T(8,128)(2,1)} custom-call(s32[192]{0:T(256)} %all_to_all.24.pairs, f32[64,64,128]{2,1,0:T(8,128)} %get-tuple-element.23.own, bf16[64,200,128]{2,1,0:T(8,128)(2,1)} %all-to-all-done.5.back, f32[8,1024]{1,0:T(8,128)} %get-tuple-element.44.share), custom_call_target="tpu_custom_call" | custom-call | tf_op jit(solution)/shard_map/collect/pallas_call | solution.py:277
  (252 shorter events, 86.1 us)
Async XLA Ops:
  2.9 20.0 %copy-start.3 = (bf16[4,4,32,1024]{3,2,1,0:T(8,128)(2,1)}, bf16[4,4,32,1024]{3,2,1,0:T(8,128)(2,1)S(1)}, u32[]{:S(2)}) copy-start(bf16[4,4,32,1024]{3,2,1,0:T(8,128)(2,1)S(1)} %reshape.236) | copy-start | bytes 3145732
  3.1 9.6 %collective-permute-start = (bf16[4,4,1,1024]{3,2,1,0:T(2,128)(2,1)S(1)}, bf16[4,4,1,1024]{3,2,1,0:T(2,128)(2,1)S(1)}, u32[]{:S(2)}, u32[]{:S(2)}) collective-permute-start(bf16[4,4,1,1024]{3,2,1,0:T(2,128)(2,1)S(1)} %broadcast_select_fusion.5), channel_id=1, source_target_pairs={{0,32},{32,0},{1,33},{33,1},{2,34},{34,2},{3,35},{35,3},{4,36},{36... | collective-permute-start | bytes 98312 | tf_op jit(solution)/shard_map/ppermute | solution.py:434
  13.0 6.8 %collective-permute-start.1 = (bf16[4,1,34,1024]{3,2,1,0:T(8,128)(2,1)S(1)}, bf16[4,1,34,1024]{3,2,1,0:T(8,128)(2,1)S(1)}, u32[]{:S(2)}, u32[]{:S(2)}) collective-permute-start(bf16[4,1,34,1024]{3,2,1,0:T(8,128)(2,1)S(1)} %get-tuple-element.36), channel_id=1, source_target_pairs={{0,1},{1,2},{2,3},{3,4},{4,5},{5,6},{6,7},{7,8},{8,9},{9,10},{10,1... | collective-permute-start | bytes 835592 | tf_op jit(solution)/shard_map/ppermute | solution.py:444
  15.8 6.8 %collective-permute-start.2 = (bf16[4,1,34,1024]{3,2,1,0:T(8,128)(2,1)S(1)}, bf16[4,1,34,1024]{3,2,1,0:T(8,128)(2,1)S(1)}, u32[]{:S(2)}, u32[]{:S(2)}) collective-permute-start(bf16[4,1,34,1024]{3,2,1,0:T(8,128)(2,1)S(1)} %get-tuple-element.37), channel_id=1, source_target_pairs={{1,0},{2,1},{3,2},{4,3},{5,4},{6,5},{7,6},{8,7},{9,8},{10,9},{11,1... | collective-permute-start | bytes 835592 | tf_op jit(solution)/shard_map/ppermute | solution.py:446
  24.7 35.8 %collective-permute-start.3 = (bf16[2,6,34,1024]{3,0,2,1:T(2,128)(2,1)}, bf16[2,6,34,1024]{3,0,2,1:T(2,128)(2,1)S(1)}, u32[]{:S(2)}, u32[]{:S(2)}) collective-permute-start(bf16[2,6,34,1024]{3,0,2,1:T(2,128)(2,1)} %copy.61), channel_id=1, source_target_pairs={{0,8},{1,9},{2,10},{3,11},{4,12},{5,13},{6,14},{7,15},{8,16},{9,17... | collective-permute-start | bytes 2506760 | tf_op jit(solution)/shard_map/ppermute | solution.py:456
  26.3 34.1 %copy-start.75 = (pred[512]{0:T(512)(128)(4,1)}, pred[512]{0:T(512)(128)(4,1)S(1)}, u32[]{:S(2)}) copy-start(pred[512]{0:T(512)(128)(4,1)S(1)} %reshape.233) | copy-start | bytes 1540
  30.7 22.6 %all-to-all-start = ((s32[64,3,1]{1,2,0:T(1,128)}), s32[64,3,1]{1,2,0:T(1,128)S(1)}, u32[]{:S(2)}, u32[]{:S(2)}) async-start(s32[64,3,1]{1,2,0:T(1,128)} %copy.59), calls=%async_computation | async-start | bytes 65536 | tf_op jit(solution)/shard_map/all_to_all | solution.py:537
  55.3 5.5 %copy-start.4 = (bf16[4,4,32,1024]{3,2,1,0:T(8,128)(2,1)S(1)}, bf16[4,4,32,1024]{3,2,1,0:T(8,128)(2,1)}, u32[]{:S(2)}) copy-start(bf16[4,4,32,1024]{3,2,1,0:T(8,128)(2,1)} %copy-done.3) | copy-start | bytes 3145732
  55.3 5.5 %copy-start.10 = (bf16[4,1,34,1024]{3,2,1,0:T(8,128)(2,1)S(1)}, bf16[4,1,34,1024]{3,2,1,0:T(8,128)(2,1)}, u32[]{:S(2)}) copy-start(bf16[4,1,34,1024]{3,2,1,0:T(8,128)(2,1)} %copy-done.9) | copy-start | bytes 835588
  61.8 12.6 %copy-start = (bf16[6,6,34,1024]{3,2,1,0:T(8,128)(2,1)}, bf16[6,6,34,1024]{3,2,1,0:T(8,128)(2,1)S(1)}, u32[]{:S(2)}) copy-start(bf16[6,6,34,1024]{3,2,1,0:T(8,128)(2,1)S(1)} %maximum_maximum_fusion.1.framed) | copy-start | bytes 7520260
  61.8 78.5 %all-to-all-start.1 = ((bf16[64,192,128]{2,1,0:T(8,128)(2,1)}), bf16[64,192,128]{2,1,0:T(8,128)(2,1)}, u32[]{:S(2)}, u32[]{:S(2)}) async-start(bf16[64,192,128]{2,1,0:T(8,128)(2,1)} %gather_pairs.2), calls=%async_computation.1 | async-start | bytes 6291456 | tf_op jit(solution)/shard_map/all_to_all | solution.py:537
  93.0 54.3 %copy-start.72 = (pred[4096]{0:T(1024)(128)(4,1)S(1)}, pred[4096]{0:T(1024)(128)(4,1)}, u32[]{:S(2)}) copy-start(pred[4096]{0:T(1024)(128)(4,1)} %copy-done.71) | copy-start | bytes 12292
  93.0 54.3 %copy-start.74 = (s32[512]{0:T(512)S(1)}, s32[512]{0:T(512)}, u32[]{:S(2)}) copy-start(s32[512]{0:T(512)} %copy-done.73) | copy-start | bytes 6148
  93.0 54.3 %copy-start.76 = (pred[512]{0:T(512)(128)(4,1)S(1)}, pred[512]{0:T(512)(128)(4,1)}, u32[]{:S(2)}) copy-start(pred[512]{0:T(512)(128)(4,1)} %copy-done.75) | copy-start | bytes 1540
  140.3 90.4 %all-to-all-start.2 = ((bf16[64,224,128]{2,1,0:T(8,128)(2,1)}), bf16[64,224,128]{2,1,0:T(8,128)(2,1)}, u32[]{:S(2)}, u32[]{:S(2)}) async-start(bf16[64,224,128]{2,1,0:T(8,128)(2,1)} %gather_pairs.3), calls=%async_computation.2 | async-start | bytes 7340032 | tf_op jit(solution)/shard_map/all_to_all | solution.py:537
  236.0 82.1 %all-to-all-start.3 = ((bf16[64,200,128]{2,1,0:T(8,128)(2,1)}), bf16[64,200,128]{2,1,0:T(8,128)(2,1)S(1)}, u32[]{:S(2)}, u32[]{:S(2)}) async-start(bf16[64,200,128]{2,1,0:T(8,128)(2,1)} %coarse_head.1), calls=%async_computation.3 | async-start | bytes 6553600 | tf_op jit(solution)/shard_map/all_to_all | solution.py:537
  332.4 23.0 %copy-start.1 = (f32[4,4,32,1024]{3,2,1,0:T(8,128)}, f32[4,4,32,1024]{3,2,1,0:T(8,128)S(1)}, u32[]{:S(2)}) copy-start(f32[4,4,32,1024]{3,2,1,0:T(8,128)S(1)} %reshape.248.grad) | copy-start | bytes 6291460
  332.5 7.2 %collective-permute-start.4 = (bf16[4,4,1,1024]{3,2,1,0:T(2,128)(2,1)S(1)}, bf16[4,4,1,1024]{3,2,1,0:T(2,128)(2,1)S(1)}, u32[]{:S(2)}, u32[]{:S(2)}) collective-permute-start(bf16[4,4,1,1024]{3,2,1,0:T(2,128)(2,1)S(1)} %fusion.37), channel_id=1, source_target_pairs={{0,32},{32,0},{1,33},{33,1},{2,34},{34,2},{3,35},{35,3},{4,36},{36... | collective-permute-start | bytes 98312 | tf_op jit(solution)/shard_map/ppermute | solution.py:434
  340.4 11.4 %collective-permute-start.5 = (f32[4,1,34,1024]{3,0,2,1:T(4,128)S(1)}, f32[4,1,34,1024]{3,0,2,1:T(4,128)S(1)}, u32[]{:S(2)}, u32[]{:S(2)}) collective-permute-start(f32[4,1,34,1024]{3,0,2,1:T(4,128)S(1)} %copy.71), channel_id=1, source_target_pairs={{0,1},{1,2},{2,3},{3,4},{4,5},{5,6},{6,7},{7,8},{8,9},{9,10},{10,1... | collective-permute-start | bytes 1671176 | tf_op jit(solution)/shard_map/ppermute | solution.py:444
  345.7 9.3 %collective-permute-start.6 = (f32[4,1,34,1024]{3,0,2,1:T(4,128)S(1)}, f32[4,1,34,1024]{3,0,2,1:T(4,128)S(1)}, u32[]{:S(2)}, u32[]{:S(2)}) collective-permute-start(f32[4,1,34,1024]{3,0,2,1:T(4,128)S(1)} %copy.73), channel_id=1, source_target_pairs={{1,0},{2,1},{3,2},{4,3},{5,4},{6,5},{7,6},{8,7},{9,8},{10,9},{11,1... | collective-permute-start | bytes 1671176 | tf_op jit(solution)/shard_map/ppermute | solution.py:446
  357.5 32.7 %collective-permute-start.7 = (bf16[2,6,34,1024]{3,0,2,1:T(2,128)(2,1)}, bf16[2,6,34,1024]{3,0,2,1:T(2,128)(2,1)}, u32[]{:S(2)}, u32[]{:S(2)}) collective-permute-start(bf16[2,6,34,1024]{3,0,2,1:T(2,128)(2,1)} %copy.75), channel_id=1, source_target_pairs={{0,56},{1,57},{2,58},{3,59},{4,60},{5,61},{6,62},{7,63},{8,0},{9,1... | collective-permute-start | bytes 2506760 | tf_op jit(solution)/shard_map/ppermute | solution.py:456
  366.8 20.8 %all-to-all-start.4 = ((f32[64,4,128]{2,1,0:T(4,128)}), f32[64,4,128]{2,1,0:T(4,128)S(1)}, u32[]{:S(2)}, u32[]{:S(2)}) async-start(f32[64,4,128]{2,1,0:T(4,128)} %reshape.249), calls=%async_computation.4 | async-start | bytes 262144 | tf_op jit(solution)/shard_map/all_to_all | solution.py:537
  395.0 81.0 %all-to-all-start.5 = ((bf16[64,200,128]{2,1,0:T(8,128)(2,1)}), bf16[64,200,128]{2,1,0:T(8,128)(2,1)}, u32[]{:S(2)}, u32[]{:S(2)}) async-start(bf16[64,200,128]{2,1,0:T(8,128)(2,1)} %sum_taps.1), calls=%async_computation.5 | async-start | bytes 6553600 | tf_op jit(solution)/shard_map/all_to_all | solution.py:537
  403.7 5.0 %slice-start = ((s8[5898240]{0:T(1024)(128)(4,1)}), s8[4194304]{0:T(1024)(128)(4,1)S(1)}, s32[]{:S(2)}) async-start(s8[5898240]{0:T(1024)(128)(4,1)} %bitcast.107), calls=%async_computation.6 | async-start | bytes 8388608
  (69 other events, 127.4 us)

commit v2 on v1

--- a/solution.py
+++ b/solution.py
@@ -130,8 +130,12 @@
         for i, r in enumerate(rs):
             acc[r] += part[64 * i : 64 * i + 64]
 
-    for h in range(HEADS):
-        one_head(h)
+    def two_heads(i, carry):
+        one_head(2 * i)
+        one_head(2 * i + 1)
+        return carry
+
+    lax.fori_loop(0, HEADS // 2, two_heads, 0)
 
     @pl.when(cube == pl.num_programs(0) - 1)
     def _():
@@ -200,8 +204,12 @@
         for i, r in enumerate(rs):
             acc[r] += part[64 * i : 64 * i + 64]
 
-    for h in range(HEADS):
-        one_head(h)
+    def two_heads(i, carry):
+        one_head(2 * i)
+        one_head(2 * i + 1)
+        return carry
+
+    lax.fori_loop(0, HEADS // 2, two_heads, 0)
 
     @pl.when(cube == pl.num_programs(0) - 1)
     def _():
@@ -253,12 +261,13 @@
     )(rows, query, grad, keys, far_keys, values, far_values, weights)
 
 
-def collect_body(pairs, own, back, share, out, acc):
+def collect_body(pairs, own, back, trailer, out, acc, *, quantity):
+    slots = pairs.shape[0] // back.shape[0]
     for p in range(own.shape[0]):
         c, h = p // HEADS, p % HEADS
-        acc[cube_rows(c), head_lanes(h)] = own[p] + share[c : c + 1, head_lanes(h)] * (1.0 / 64.0)
-
-    slots = pairs.shape[0] // back.shape[0]
+        high = trailer[p, quantity : quantity + 1].astype(F32)
+        low = trailer[p, TRAILER // 2 + quantity : TRAILER // 2 + quantity + 1].astype(F32)
+        acc[cube_rows(c), head_lanes(h)] = own[p] + (high + low) * (1.0 / 64.0)
 
     def one(d, carry):
         for s in range(slots):
@@ -269,24 +278,44 @@
         return carry
 
     lax.fori_loop(0, back.shape[0], one, 0)
-    out[...] = acc[...].astype(out.dtype)
-
-
-def collect(pairs, own, back, share, dtype):
-    shape = (own.shape[0] // HEADS * 64, HEADS * HEAD_DIM)
+    if len(out.shape) == 2:
+        out[...] = acc[...].astype(out.dtype)
+        return
+
+    def lane_block(h, carry):
+        lanes = head_lanes(h)
+        for g in range(acc.shape[0] // 64):
+            for i in range(16):
+                row = 64 * g + 4 * i
+                out[i // 4, i % 4, 4 * g : 4 * g + 4, lanes] = acc[row : row + 4, lanes]
+        return carry
+
+    lax.fori_loop(0, HEADS, lane_block, 0)
+
+
+def collect(pairs, own, back, halves, quantity, lattice):
+    cubes = own.shape[0] // HEADS
+    width = HEADS * HEAD_DIM
+    tokens = (cubes * 64, width)
+    shape, dtype = ((4, 4, 4 * cubes, width), F32) if lattice else (tokens, BF)
+    last = halves.shape[1] // TRAILER - 1
     return pl.pallas_call(
-        collect_body,
+        functools.partial(collect_body, quantity=quantity),
         grid_spec=pltpu.PrefetchScalarGridSpec(
             num_scalar_prefetch=1,
             grid=(1,),
-            in_specs=[whole(own.shape), whole(back.shape), whole(share.shape)],
+            in_specs=[
+                whole(own.shape),
+                whole(back.shape),
+                pl.BlockSpec((halves.shape[0], TRAILER, HEAD_DIM), lambda *_: (0, last, 0)),
+            ],
             out_specs=whole(shape),
-            scratch_shapes=[pltpu.VMEM(shape, F32)],
+            scratch_shapes=[pltpu.VMEM(tokens, F32)],
         ),
         out_shape=jax.ShapeDtypeStruct(shape, dtype),
         compiler_params=VMEM,
         name="collect",
-    )(pairs, own, back, share)
+    )(pairs, own, back, halves)
 
 
 def put_halves(target, sem, stage, parts):
@@ -369,8 +398,9 @@
                             term = jnp.sum((grad[f, y] * cells).reshape(-1, 8, 128), axis=0)
                             sums[tap] = sums[tap] + term if tap in sums else term
         for tap, total in sums.items():
-            out[tap : tap + 1] = jnp.sum(total, axis=0, keepdims=True)
-    out[27:] = jnp.zeros((out.shape[0] - 27, 128), F32)
+            out[tap // 4, 0, tap % 4 : tap % 4 + 1] = jnp.sum(total, axis=0, keepdims=True)
+    out[6, 0, 3:] = jnp.zeros((1, 128), F32)
+    out[7, 0] = jnp.zeros((4, 128), F32)
 
 
 def tap_gradients(grad, framed):
@@ -382,9 +412,9 @@
             pl.BlockSpec(grad.shape[:3] + (128,), lambda i: (0, 0, 0, i)),
             pl.BlockSpec(framed.shape[:3] + (128,), lambda i: (0, 0, 0, i)),
         ],
-        out_specs=pl.BlockSpec((32, 128), lambda i: (0, i)),
+        out_specs=pl.BlockSpec((8, 1, 4, 128), lambda i: (0, i, 0, 0)),
         scratch_shapes=[pltpu.VMEM((framed.shape[0] * framed.shape[1], 40, 128), F32)],
-        out_shape=jax.ShapeDtypeStruct((32, width), F32),
+        out_shape=jax.ShapeDtypeStruct((8, width // 128, 4, 128), F32),
         compiler_params=VMEM,
         name="tap_gradients",
     )(grad, framed)
@@ -424,36 +454,36 @@
     )(shares, back)
 
 
-def from_partner(block, axis, apart):
-    count = lax.axis_size(axis)
-    route = []
-    for low in range(count):
-        high = low | 1 << apart
-        if high != low and high < count:
-            route += [(low, high), (high, low)]
-    return lax.ppermute(block, axis, route)
-
-
-def with_halo(cells, sides, width):
-    for axis, dim in sides:
-        count = lax.axis_size(axis)
-        head = lax.slice_in_dim(cells, 0, width, axis=dim)
-        tail = lax.slice_in_dim(cells, cells.shape[dim] - width, cells.shape[dim], axis=dim)
-        cells = jnp.concatenate(
-            [
-                lax.ppermute(tail, axis, [(i, (i + 1) % count) for i in range(count)]),
-                cells,
-                lax.ppermute(head, axis, [((i + 1) % count, i) for i in range(count)]),
-            ],
-            axis=dim,
-        )
-    return cells
-
-
-def passed_along(value, axis, steps):
-    count = lax.axis_size(axis)
-    pairs = [(source, (source + steps) % count) for source in range(count)]
-    return lax.ppermute(value, axis, pairs)
+def shifted(block, steps):
+    count = lax.axis_size("seq")
+    return lax.ppermute(block, "seq", [(i, (i + steps) % count) for i in range(count)])
+
+
+def with_neighbours(lattice, forward, place, ready=None):
+    row_band, slab_index, col_half, band_count = place
+    half = lax.axis_size("seq") // 2
+    own = lattice.astype(BF)
+    edge = jnp.where(col_half == 0, own[:, :, -1:], own[:, :, :1])
+    frames = slice(-2, None) if forward else slice(0, 2)
+    steps = band_count if forward else -band_count
+    has_slab = slab_index > 0 if forward else slab_index < SLABS - 1
+    own_edge = shifted(edge, half)
+    near = shifted(own[frames], steps)
+    near_edge = shifted(edge[frames], steps + half)
+    near = jnp.where(has_slab, near, jnp.zeros_like(near)).astype(lattice.dtype)
+    near_edge = jnp.where(has_slab, near_edge, jnp.zeros_like(near_edge))
+    order = (lambda a, b: [a, b]) if forward else (lambda a, b: [b, a])
+    middle = jnp.concatenate(order(near, lattice), axis=0)
+    edges = jnp.concatenate(order(near_edge, own_edge), axis=0).astype(lattice.dtype)
+    wide = side_columns(middle, edges, col_half)
+    top, bottom = wide[:, :1].astype(BF), wide[:, -1:].astype(BF)
+    if ready is not None:
+        top, bottom = lax.optimization_barrier((top, bottom, ready))[:2]
+    above = shifted(bottom, 1)
+    below = shifted(top, -1)
+    above = jnp.where(row_band > 0, above, jnp.zeros_like(above)).astype(lattice.dtype)
+    below = jnp.where(row_band < band_count - 1, below, jnp.zeros_like(below))
+    return jnp.concatenate([above, wide, below.astype(lattice.dtype)], axis=1)
 
 
 def to_lattice(tokens):
@@ -476,13 +506,6 @@
         [jnp.where(col_half == 1, edge, blank), lattice, jnp.where(col_half == 0, edge, blank)],
         axis=2,
     )
-
-
-def clear_rims(extended, row_band, band_count):
-    blank = jnp.zeros_like(extended[:, :1])
-    upper = jnp.where(row_band > 0, extended[:, :1], blank)
-    lower = jnp.where(row_band < band_count - 1, extended[:, -1:], blank)
-    return jnp.concatenate([upper, extended[:, 1:-1], lower], axis=1)
 
 
 def convolve_values(framed, filter_taps):
@@ -537,8 +560,8 @@
     return lax.all_to_all(rows, "seq", split_axis=0, concat_axis=0, tiled=True)
 
 
-def after(value, *earlier):
-    return lax.optimization_barrier((value, *earlier))[0]
+def together(*values):
+    return lax.optimization_barrier(values)
 
 
 def shards(query_tokens, key_tokens, value_tokens, gate_tokens, filter_taps, selected, cotangent):
@@ -554,42 +577,34 @@
     row_band = rotated % band_count
     slab_index = rotated // band_count % SLABS
     col_half = rotated // (devices // 2)
-    col_bit = devices.bit_length() - 2
 
     owner_device = selected // cube_count
     pair_index = selected % cube_count * HEADS + jnp.arange(HEADS, dtype=jnp.int32)[None, :, None]
-    remote_flat = (owner_device != device_index).reshape(-1)
-    pair_codes = (owner_device * pair_count + pair_index).reshape(-1)
-    matches = (
-        pair_codes[:, None] == jnp.arange(devices * pair_count, dtype=jnp.int32)[None, :]
-    ) & remote_flat[:, None]
-    present = jnp.any(matches, axis=0).reshape(devices, pair_count).astype(jnp.int32)
-    slot_rank = jnp.cumsum(present, axis=1) - present
-    in_slot = (slot_rank[:, :, None] == jnp.arange(capacity, dtype=jnp.int32)[None, None, :]) & (
-        present[:, :, None] > 0
-    )
-    requests = jnp.sum(
-        in_slot.astype(jnp.int32) * jnp.arange(pair_count, dtype=jnp.int32)[None, :, None], axis=1
-    ).reshape(-1)
+    owner_flat, pair_flat = owner_device.reshape(-1), pair_index.reshape(-1)
+    remote_flat = owner_flat != device_index
+    of_owner = (owner_flat[:, None] == jnp.arange(devices, dtype=jnp.int32)) & remote_flat[:, None]
+    of_owner = of_owner.astype(BF)
+    pair_ids = jnp.arange(pair_count, dtype=jnp.int32)
+    of_pair = (pair_flat[:, None] == pair_ids).astype(BF)
+    present = mm(of_owner, of_pair, ((0,), (0,))) > 0.5
+    earlier = (pair_ids[:, None] < pair_ids).astype(BF)
+    slot_rank = mm(present.astype(BF), earlier, ((1,), (0,)))
+    in_slot = (slot_rank[:, None, :] == jnp.arange(capacity, dtype=F32)[None, :, None]) & (
+        present[:, None, :]
+    )
+    requests = jnp.sum(jnp.where(in_slot, pair_ids, 0), axis=2).reshape(-1)
     asked_pairs = exchanged(requests)
-    slot_of = jnp.sum(matches.astype(jnp.int32) * slot_rank.reshape(-1)[None, :], axis=1)
+    owner_rank = mm(of_owner, slot_rank.astype(BF), ((1,), (0,)))
+    slot_of = jnp.sum(owner_rank * of_pair.astype(F32), axis=1).astype(jnp.int32)
     table_row = jnp.where(
-        remote_flat,
-        pair_count + owner_device.reshape(-1) * capacity + slot_of,
-        pair_index.reshape(-1),
-    )
-
-    lattice = to_lattice(value_tokens)
-    value_edge = from_partner(
-        jnp.where(col_half == 0, lattice[:, :, -1:], lattice[:, :, :1]), "seq", col_bit
-    )
-    value_wide = side_columns(lattice, value_edge, col_half)
-    value_tall = clear_rims(with_halo(value_wide, (("seq", 1),), 1), row_band, band_count)
-    prior_frames = passed_along(value_tall[-2:], "seq", band_count)
-    prior_frames = jnp.where(slab_index > 0, prior_frames, jnp.zeros_like(prior_frames))
-    framed = jnp.concatenate([prior_frames, value_tall], axis=0)
-
-    far_keys = exchanged(after(gather_pairs(asked_pairs, key_tokens, devices), framed))
+        remote_flat, pair_count + owner_flat * capacity + slot_of, pair_flat
+    )
+
+    place = (row_band, slab_index, col_half, band_count)
+    framed = with_neighbours(to_lattice(value_tokens), True, place, asked_pairs)
+
+    asked_keys, framed = together(gather_pairs(asked_pairs, key_tokens, devices), framed)
+    far_keys = exchanged(asked_keys)
 
     filtered = from_lattice(convolve_values(framed, filter_taps)).astype(BF)
     gated = cotangent.astype(F32) * gate_tokens.astype(F32)
@@ -604,7 +619,10 @@
     )
     pooled = pooled.reshape(cube_count, 4, HEADS, HEAD_DIM).transpose(2, 1, 0, 3)
     pooled = pooled.reshape(HEADS, 4 * cube_count, HEAD_DIM)
-    far_values = exchanged(after(gather_pairs(asked_pairs, filtered, devices, pooled), far_keys))
+    asked_values, far_keys = together(
+        gather_pairs(asked_pairs, filtered, devices, pooled), far_keys
+    )
+    far_values = exchanged(asked_values)
     one_head = far_values[:, capacity * 64 :].reshape(devices, 4, cube_count, HEAD_DIM)
     one_head = one_head.transpose(1, 0, 2, 3).reshape(4, devices * cube_count, HEAD_DIM)
 
@@ -619,32 +637,24 @@
     )
     coarse = from_halves(back_value).reshape(cube_count, HEADS, 4, HEAD_DIM)
     coarse = coarse.transpose(2, 0, 1, 3).reshape(4, cube_count, channels)
-    coarse_out, coarse_query, coarse_key, coarse_value = coarse
+    coarse_out, coarse_query = coarse[:2]
 
     coarse_tokens = spread(coarse_out)
     attended = (fine_out + gate_tokens.astype(F32) * coarse_tokens).astype(BF)
     gate_gradient = (cotangent.astype(F32) * coarse_tokens).astype(BF)
     query_gradient = (fine_query + spread(coarse_query) / 64.0).astype(BF)
 
-    filtered_grad = collect(
-        asked_pairs, after(own_value, back_key), back_value, coarse_value, F32
-    )
-    grad_lattice = to_lattice(filtered_grad)
-    grad_edge = from_partner(
-        jnp.where(col_half == 0, grad_lattice[:, :, -1:], grad_lattice[:, :, :1]).astype(BF),
-        "seq",
-        col_bit,
-    ).astype(F32)
-    grad_wide = side_columns(grad_lattice, grad_edge, col_half)
-    grad_tall = clear_rims(with_halo(grad_wide, (("seq", 1),), 1), row_band, band_count)
-    next_frames = passed_along(grad_tall[:2].astype(BF), "seq", -band_count).astype(F32)
-    next_frames = jnp.where(slab_index < SLABS - 1, next_frames, jnp.zeros_like(next_frames))
-    grad_space = jnp.concatenate([grad_tall, next_frames], axis=0)
+    own_value, back_key = together(own_value, back_key)
+    grad_lattice = collect(asked_pairs, own_value, back_value, back_value, 3, True)
+    grad_space = with_neighbours(grad_lattice, False, place)
     shares = exchanged(tap_gradients(grad_lattice, framed).reshape(devices, TRAILER // 2, HEAD_DIM))
-    back_key = exchanged(after(sum_taps(shares, back_key), grad_space))
-    filter_gradient = from_halves(back_key).reshape(-1, channels)[: filter_taps.shape[0]]
+    back_key, grad_space = together(sum_taps(shares, back_key), grad_space)
+    back_key = exchanged(back_key)
+    taps = from_halves(back_key).reshape(8, HEADS, TRAILER // 2, HEAD_DIM)
+    taps = taps.transpose(0, 2, 1, 3).reshape(-1, channels)
+    filter_gradient = taps[: filter_taps.shape[0]]
     value_gradient = from_lattice(convolve_back(grad_space, filter_taps)).astype(BF)
-    key_gradient = collect(asked_pairs, own_key, back_key, coarse_key, BF)
+    key_gradient = collect(asked_pairs, own_key, back_key, back_value, 2, False)
     return (attended, query_gradient, key_gradient, value_gradient, gate_gradient, filter_gradient)
 
 

time: 494 us -> 464 us (0.939); the launches traced: 485 us -> 462 us
  waiting for transfers between devices: 254 us -> 218 us
  Pallas kernels: 86.5 us -> 111 us
  local copies, waits for them, and re-layouts: 26.9 us -> 16.6 us
  other arithmetic: 48.6 us -> 41.1 us
  starting transfers between devices: 65.9 us -> 73 us
    all_to_all x6, waiting for transfers between devices: 232 us -> 209 us  [exchanged(): return lax.all_to_all(rows, 'seq', split_axis=0, concat_axis=0, tiled=True)]
    pallas_call x1, Pallas kernels: 21.1 us -> 40.5 us  [fine_probs(): pl.pallas_call(functools.partial(probs_body, scale=scale, pairs=pairs, sl...]
    ppermute x8 -> x10, waiting for transfers between devices: 22.2 us -> 9.41 us  [shifted(): lax.ppermute(block, 'seq', [(i, (i + steps) % count) for i in range(count)])]
    ppermute x8 -> x10, starting transfers between devices: 19.5 us -> 25.8 us  [shifted(): lax.ppermute(block, 'seq', [(i, (i + steps) % count) for i in range(count)])]
  transfers between devices with their start and end apart: 14 -> 16, of which waited for: 12 -> 11; matrix products, arithmetic and copies ran while one was open for 10% -> 8% of each run, Pallas kernels for 14% -> 20%
where the time goes in v2:
time: 464 us; the launch traced here: 462 us
  waiting for transfers between devices  218 us (47%)
  Pallas kernels  111 us (24%)
  starting transfers between devices  73 us (16%)
  other arithmetic  41.1 us (9%)
  local copies, waits for them, and re-layouts  16.6 us (4%)
    all_to_all x6, waiting for transfers between devices, exchanged(): return lax.all_to_all(rows, 'seq', split_axis=0, concat_axis=0, tiled=True)  209 us
    all_to_all x6, starting transfers between devices, exchanged(): return lax.all_to_all(rows, 'seq', split_axis=0, concat_axis=0, tiled=True)  47.2 us
    pallas_call x1, Pallas kernels, fine_probs(): pl.pallas_call(functools.partial(probs_body, scale=scale, pairs=pairs, sl...  40.5 us
    pallas_call x1, Pallas kernels, fine_grads(): pl.pallas_call(functools.partial(grads_body, scale=scale, pairs=pairs, sl...  33.2 us
    ppermute x10, starting transfers between devices, shifted(): lax.ppermute(block, 'seq', [(i, (i + steps) % count) for i in range(count)])  25.8 us
    pallas_call x2, Pallas kernels, collect(): pl.pallas_call(functools.partial(collect_body, quantity=quantity), grid_s...  14.1 us
    reduce_sum x4, other arithmetic, pool_cubes(): jnp.mean(tokens.astype(jnp.float32).reshape(tokens.shape[0] // 64, 64, to...  11.7 us
    pallas_call x2, Pallas kernels, gather_pairs(): pl.pallas_call(functools.partial(gather_body, dests=dests, slots=slots),...  10.3 us
  transfers between devices with their start and end apart: 16, of which 11 were waited for; matrix products, arithmetic and copies ran while one was open for 8% of the time, Pallas kernels for 20%

profile of v2, /device:TPU:1, one launch (start us, length us, event | category | flops | bytes accessed | tf_op | source)
XLA Modules:
  0.0 462.2 jit_solution(14117113067620937411)
XLA Ops:
  6.0 5.6 %collective-permute-start = (bf16[2,4,1,1024]{3,2,1,0:T(2,128)(2,1)S(1)}, bf16[2,4,1,1024]{3,2,1,0:T(2,128)(2,1)S(1)}, u32[]{:S(2)}, u32[]{:S(2)}) collective-permute-start(bf16[2,4,1,1024]{3,2,1,0:T(2,128)(2,1)S(1)} %slice.449), channel_id=1, source_target_pairs={{0,40},{1,41},{2,42},{3,43},{4,44},{5,45},{6,46},{7,47},{8,48},{9,... | collective-permute-start | bytes 49160 | tf_op jit(solution)/shard_map/ppermute | solution.py:459
  13.2 8.2 %all-to-all-start = ((s32[64,3,1]{1,2,0:T(1,128)}), s32[64,3,1]{1,2,0:T(1,128)S(1)}, u32[]{:S(2)}, u32[]{:S(2)}) async-start(s32[64,3,1]{1,2,0:T(1,128)} %copy.39), calls=%async_computation | async-start | bytes 65536 | tf_op jit(solution)/shard_map/all_to_all | solution.py:560
  21.4 5.5 %collective-permute-start.1 = (bf16[4,4,1,1024]{3,2,1,0:T(2,128)(2,1)S(1)}, bf16[4,4,1,1024]{3,2,1,0:T(2,128)(2,1)S(1)}, u32[]{:S(2)}, u32[]{:S(2)}) collective-permute-start(bf16[4,4,1,1024]{3,2,1,0:T(2,128)(2,1)S(1)} %broadcast_select_fusion.8), channel_id=1, source_target_pairs={{0,32},{1,33},{2,34},{3,35},{4,36},{5,37},{6,38},{7,39},{8,40},{9,... | collective-permute-start | bytes 98312 | tf_op jit(solution)/shard_map/ppermute | solution.py:459
  35.7 5.2 %gather_pairs.2 = bf16[64,192,128]{2,1,0:T(8,128)(2,1)} custom-call(s32[192]{0:T(256)} %all_to_all.24.pairs, bf16[512,1024]{1,0:T(8,128)(2,1)} %keys.3), custom_call_target="tpu_custom_call" | custom-call | tf_op jit(solution)/shard_map/gather_pairs/pallas_call | solution.py:60
  46.4 9.9 %all-to-all-start.1 = ((bf16[64,192,128]{2,1,0:T(8,128)(2,1)}), bf16[64,192,128]{2,1,0:T(8,128)(2,1)}, u32[]{:S(2)}, u32[]{:S(2)}) async-start(bf16[64,192,128]{2,1,0:T(8,128)(2,1)} %gather_pairs.2), calls=%async_computation.1 | async-start | bytes 6291456 | tf_op jit(solution)/shard_map/all_to_all | solution.py:560
  60.0 8.6 %convert_reduce_fusion.2 = (f32[32,1024]{1,0:T(8,128)S(1)}, bf16[4,4,32,1024]{3,2,1,0:T(8,128)(2,1)}) fusion(bf16[6,6,34,1024]{3,2,1,0:T(8,128)(2,1)S(1)} %pad_maximum_fusion.1.framed, f32[1024]{0:T(1024)S(1)} %bitcast.142, f32[1024]{0:T(1024)S(1)} %bitcast.144, f32[1024]{0:T(1024)S(1)} %bitcast.148, f32[1024]{0:T(1024)S(1)} %bitcast.150, ...), kind=kLoop, calls=%fused_computation.14 | loop fusion | flops 43483136 | bytes 29601792 | tf_op jit(solution)/shard_map/reduce_sum | solution.py:547
  72.5 5.2 %gather_pairs.3 = bf16[64,224,128]{2,1,0:T(8,128)(2,1)} custom-call(s32[192]{0:T(256)} %all_to_all.24.pairs, bf16[512,1024]{1,0:T(8,128)(2,1)} %convert_element_type.268.tokens.values, bf16[8,32,128]{2,1,0:T(8,128)(2,1)} %maximum_bitcast_fusion.rest_0_), custom_call_target="tpu_custom_call" | custom-call | tf_op jit(solution)/shard_map/gather_pairs/pallas_call | solution.py:60
  77.7 51.0 %all-to-all-done.1.far_keys = bf16[64,192,128]{2,1,0:T(8,128)(2,1)} async-done(((bf16[64,192,128]{2,1,0:T(8,128)(2,1)}), bf16[64,192,128]{2,1,0:T(8,128)(2,1)}, u32[]{:S(2)}, u32[]{:S(2)}) %all-to-all-start.1) | async-done | bytes 3145760 | tf_op jit(solution)/shard_map/all_to_all | solution.py:560
  128.7 6.9 %all-to-all-start.2 = ((bf16[64,224,128]{2,1,0:T(8,128)(2,1)}), bf16[64,224,128]{2,1,0:T(8,128)(2,1)}, u32[]{:S(2)}, u32[]{:S(2)}) async-start(bf16[64,224,128]{2,1,0:T(8,128)(2,1)} %gather_pairs.3), calls=%async_computation.2 | async-start | bytes 7340032 | tf_op jit(solution)/shard_map/all_to_all | solution.py:560
  136.6 40.5 %fine_probs.1 = (f32[64,64,512]{2,1,0:T(8,128)}, f32[64,64,128]{2,1,0:T(8,128)}, bf16[64,200,128]{2,1,0:T(8,128)(2,1)}) custom-call(s32[512]{0:T(512)} %add_select_fusion.2.rows, bf16[512,1024]{1,0:T(8,128)(2,1)} %query.3, bf16[512,1024]{1,0:T(8,128)(2,1)} %grad.3, bf16[512,1024]{1,0:T(8,128)(2,1)} %keys.3, bf16[64,192,128]{2,1,0:T(8,128)(2,1)} %all-to-all-done.1.far_keys), custom_call_target="tpu_custom_call" | custom-call | tf_op jit(solution)/shard_map/fine_probs/pallas_call | solution.py:152
  177.1 42.3 %all-to-all-done.2.far_values = bf16[64,224,128]{2,1,0:T(8,128)(2,1)} async-done(((bf16[64,224,128]{2,1,0:T(8,128)(2,1)}), bf16[64,224,128]{2,1,0:T(8,128)(2,1)}, u32[]{:S(2)}, u32[]{:S(2)}) %all-to-all-start.2) | async-done | bytes 3670048 | tf_op jit(solution)/shard_map/all_to_all | solution.py:560
  224.6 6.7 %all-to-all-start.3 = ((bf16[64,200,128]{2,1,0:T(8,128)(2,1)}), bf16[64,200,128]{2,1,0:T(8,128)(2,1)S(1)}, u32[]{:S(2)}, u32[]{:S(2)}) async-start(bf16[64,200,128]{2,1,0:T(8,128)(2,1)} %coarse_head.1), calls=%async_computation.3 | async-start | bytes 6553600 | tf_op jit(solution)/shard_map/all_to_all | solution.py:560
  231.3 33.2 %fine_grads.1 = (f32[512,1024]{1,0:T(8,128)}, f32[512,1024]{1,0:T(8,128)}, f32[64,64,128]{2,1,0:T(8,128)}, bf16[64,200,128]{2,1,0:T(8,128)(2,1)}) custom-call(s32[512]{0:T(512)} %add_select_fusion.2.rows, bf16[512,1024]{1,0:T(8,128)(2,1)} %query.3, bf16[512,1024]{1,0:T(8,128)(2,1)} %grad.3, bf16[512,1024]{1,0:T(8,128)(2,1)} %keys.3, ...), custom_call_target="tpu_custom_call" | custom-call | tf_op jit(solution)/shard_map/fine_grads/pallas_call | solution.py:227
  264.5 42.0 %all-to-all-done.3.back.trailer = bf16[64,200,128]{2,1,0:T(8,128)(2,1)S(1)} async-done(((bf16[64,200,128]{2,1,0:T(8,128)(2,1)}), bf16[64,200,128]{2,1,0:T(8,128)(2,1)S(1)}, u32[]{:S(2)}, u32[]{:S(2)}) %all-to-all-start.3) | async-done | bytes 3276832 | tf_op jit(solution)/shard_map/all_to_all | solution.py:560
  308.2 7.4 %collect.2.grad = f32[4,4,32,1024]{3,2,1,0:T(8,128)} custom-call(s32[192]{0:T(256)} %all_to_all.24.pairs, f32[64,64,128]{2,1,0:T(8,128)} %get-tuple-element.36.own, bf16[64,200,128]{2,1,0:T(8,128)(2,1)} %copy-done.1, bf16[64,200,128]{2,1,0:T(8,128)(2,1)} %copy-done.1), custom_call_target="tpu_custom_call" | custom-call | tf_op jit(solution)/shard_map/collect/pallas_call | solution.py:302
  319.1 5.4 %collective-permute-start.5 = (bf16[4,4,1,1024]{3,2,1,0:T(2,128)(2,1)S(1)}, bf16[4,4,1,1024]{3,2,1,0:T(2,128)(2,1)S(1)}, u32[]{:S(2)}, u32[]{:S(2)}) collective-permute-start(bf16[4,4,1,1024]{3,2,1,0:T(2,128)(2,1)S(1)} %broadcast_select_fusion.7), channel_id=1, source_target_pairs={{0,32},{1,33},{2,34},{3,35},{4,36},{5,37},{6,38},{7,39},{8,40},{9,... | collective-permute-start | bytes 98312 | tf_op jit(solution)/shard_map/ppermute | solution.py:459
  324.9 4.8 %collective-permute-done.5 = bf16[4,4,1,1024]{3,2,1,0:T(2,128)(2,1)S(1)} collective-permute-done((bf16[4,4,1,1024]{3,2,1,0:T(2,128)(2,1)S(1)}, bf16[4,4,1,1024]{3,2,1,0:T(2,128)(2,1)S(1)}, u32[]{:S(2)}, u32[]{:S(2)}) %collective-permute-start.5) | collective-permute-done | bytes 32800 | tf_op jit(solution)/shard_map/ppermute | solution.py:459
  337.0 7.7 %tap_gradients.1 = f32[8,8,4,128]{3,2,1,0:T(4,128)} custom-call(f32[4,4,32,1024]{3,2,1,0:T(8,128)} %collect.2.grad, bf16[6,6,34,1024]{3,2,1,0:T(8,128)(2,1)} %copy-done), custom_call_target="tpu_custom_call" | custom-call | tf_op jit(solution)/shard_map/tap_gradients/pallas_call | solution.py:408
  344.7 10.0 %all-to-all-start.4 = ((f32[64,4,128]{2,1,0:T(4,128)}), f32[64,4,128]{2,1,0:T(4,128)S(1)}, u32[]{:S(2)}, u32[]{:S(2)}) async-start(f32[64,4,128]{2,1,0:T(4,128)} %bitcast.120), calls=%async_computation.4 | async-start | bytes 262144 | tf_op jit(solution)/shard_map/all_to_all | solution.py:560
  355.3 10.6 %all-to-all-done.4.shares = f32[64,4,128]{2,1,0:T(4,128)S(1)} async-done(((f32[64,4,128]{2,1,0:T(4,128)}), f32[64,4,128]{2,1,0:T(4,128)S(1)}, u32[]{:S(2)}, u32[]{:S(2)}) %all-to-all-start.4) | async-done | bytes 131104 | tf_op jit(solution)/shard_map/all_to_all | solution.py:560
  373.0 5.5 %all-to-all-start.5 = ((bf16[64,200,128]{2,1,0:T(8,128)(2,1)}), bf16[64,200,128]{2,1,0:T(8,128)(2,1)}, u32[]{:S(2)}, u32[]{:S(2)}) async-start(bf16[64,200,128]{2,1,0:T(8,128)(2,1)} %sum_taps.1), calls=%async_computation.5 | async-start | bytes 6553600 | tf_op jit(solution)/shard_map/all_to_all | solution.py:560
  384.9 7.8 %add_convert_fusion = bf16[4,4,32,1024]{3,2,1,0:T(8,128)(2,1)S(1)} fusion(f32[6,6,34,1024]{3,2,1,0:T(8,128)S(1)} %bitcast.115, f32[1024]{0:T(1024)S(1)} %bitcast.143, f32[1024]{0:T(1024)S(1)} %bitcast.145, f32[1024]{0:T(1024)S(1)} %bitcast.149, f32[1024]{0:T(1024)S(1)} %bitcast.151, f32[1024]{0:T(1024)S(1)} %bitcast.153, f32[1024]{0:T(1024)S(1)} %bitcast.155, ...), kind=kLoop, calls=%fused_computation.13 | loop fusion | flops 28311552 | bytes 57782272 | tf_op jit(solution)/shard_map/convert_element_type | solution.py:656
  394.8 59.1 %all-to-all-done.5.back = bf16[64,200,128]{2,1,0:T(8,128)(2,1)} async-done(((bf16[64,200,128]{2,1,0:T(8,128)(2,1)}), bf16[64,200,128]{2,1,0:T(8,128)(2,1)}, u32[]{:S(2)}, u32[]{:S(2)}) %all-to-all-start.5) | async-done | bytes 3276832 | tf_op jit(solution)/shard_map/all_to_all | solution.py:560
  455.6 6.6 %collect.3 = bf16[512,1024]{1,0:T(8,128)(2,1)} custom-call(s32[192]{0:T(256)} %all_to_all.24.pairs, f32[64,64,128]{2,1,0:T(8,128)} %get-tuple-element.33.own, bf16[64,200,128]{2,1,0:T(8,128)(2,1)} %all-to-all-done.5.back, bf16[64,200,128]{2,1,0:T(8,128)(2,1)} %copy-done.1), custom_call_target="tpu_custom_call" | custom-call | tf_op jit(solution)/shard_map/collect/pallas_call | solution.py:302
  (125 shorter events, 65.2 us)
Async XLA Ops:
  2.6 9.0 %copy-start.16 = (s32[8,8,8]{2,1,0:T(8,128)S(1)}, s32[8,8,8]{2,1,0:T(8,128)}, u32[]{:S(2)}) copy-start(s32[8,8,8]{2,1,0:T(8,128)} %param.12) | copy-start | bytes 6148
  3.0 30.2 %collective-permute-start.2 = (bf16[2,4,32,1024]{3,2,1,0:T(8,128)(2,1)S(1)}, bf16[2,4,32,1024]{3,2,1,0:T(8,128)(2,1)}, u32[]{:S(2)}, u32[]{:S(2)}) collective-permute-start(bf16[2,4,32,1024]{3,2,1,0:T(8,128)(2,1)S(1)} %slice.350), channel_id=1, source_target_pairs={{0,8},{1,9},{2,10},{3,11},{4,12},{5,13},{6,14},{7,15},{8,16},{9,17... | collective-permute-start | bytes 1572872 | tf_op jit(solution)/shard_map/ppermute | solution.py:459
  5.8 29.0 %copy-start.6 = (bf16[4,4,32,1024]{3,2,1,0:T(8,128)(2,1)}, bf16[4,4,32,1024]{3,2,1,0:T(8,128)(2,1)S(1)}, u32[]{:S(2)}) copy-start(bf16[4,4,32,1024]{3,2,1,0:T(8,128)(2,1)S(1)} %reshape.315) | copy-start | bytes 3145732
  6.0 26.9 %collective-permute-start = (bf16[2,4,1,1024]{3,2,1,0:T(2,128)(2,1)S(1)}, bf16[2,4,1,1024]{3,2,1,0:T(2,128)(2,1)S(1)}, u32[]{:S(2)}, u32[]{:S(2)}) collective-permute-start(bf16[2,4,1,1024]{3,2,1,0:T(2,128)(2,1)S(1)} %slice.449), channel_id=1, source_target_pairs={{0,40},{1,41},{2,42},{3,43},{4,44},{5,45},{6,46},{7,47},{8,48},{9,... | collective-permute-start | bytes 49160 | tf_op jit(solution)/shard_map/ppermute | solution.py:459
  13.2 17.7 %all-to-all-start = ((s32[64,3,1]{1,2,0:T(1,128)}), s32[64,3,1]{1,2,0:T(1,128)S(1)}, u32[]{:S(2)}, u32[]{:S(2)}) async-start(s32[64,3,1]{1,2,0:T(1,128)} %copy.39), calls=%async_computation | async-start | bytes 65536 | tf_op jit(solution)/shard_map/all_to_all | solution.py:560
  21.4 11.5 %collective-permute-start.1 = (bf16[4,4,1,1024]{3,2,1,0:T(2,128)(2,1)S(1)}, bf16[4,4,1,1024]{3,2,1,0:T(2,128)(2,1)S(1)}, u32[]{:S(2)}, u32[]{:S(2)}) collective-permute-start(bf16[4,4,1,1024]{3,2,1,0:T(2,128)(2,1)S(1)} %broadcast_select_fusion.8), channel_id=1, source_target_pairs={{0,32},{1,33},{2,34},{3,35},{4,36},{5,37},{6,38},{7,39},{8,40},{9,... | collective-permute-start | bytes 98312 | tf_op jit(solution)/shard_map/ppermute | solution.py:459
  33.2 7.7 %copy-start.11 = (bf16[6,4,1,1024]{3,2,1,0:T(2,128)(2,1)}, bf16[6,4,1,1024]{3,2,1,0:T(2,128)(2,1)S(1)}, u32[]{:S(2)}) copy-start(bf16[6,4,1,1024]{3,2,1,0:T(2,128)(2,1)S(1)} %get-tuple-element.81) | copy-start | bytes 147460
  34.8 6.7 %collective-permute-start.3 = (bf16[6,1,34,1024]{3,2,1,0:T(8,128)(2,1)S(1)}, bf16[6,1,34,1024]{3,2,1,0:T(8,128)(2,1)S(1)}, u32[]{:S(2)}, u32[]{:S(2)}) collective-permute-start(bf16[6,1,34,1024]{3,2,1,0:T(8,128)(2,1)S(1)} %get-tuple-element.23), channel_id=1, source_target_pairs={{0,1},{1,2},{2,3},{3,4},{4,5},{5,6},{6,7},{7,8},{8,9},{9,10},{10,1... | collective-permute-start | bytes 1253384 | tf_op jit(solution)/shard_map/ppermute | solution.py:459
  35.7 8.6 %collective-permute-start.4 = (bf16[6,1,34,1024]{3,2,1,0:T(8,128)(2,1)S(1)}, bf16[6,1,34,1024]{3,2,1,0:T(8,128)(2,1)S(1)}, u32[]{:S(2)}, u32[]{:S(2)}) collective-permute-start(bf16[6,1,34,1024]{3,2,1,0:T(8,128)(2,1)S(1)} %get-tuple-element.24), channel_id=1, source_target_pairs={{0,63},{1,0},{2,1},{3,2},{4,3},{5,4},{6,5},{7,6},{8,7},{9,8},{10,9... | collective-permute-start | bytes 1253384 | tf_op jit(solution)/shard_map/ppermute | solution.py:459
  35.7 8.6 %copy-start.7 = (bf16[4,4,32,1024]{3,2,1,0:T(8,128)(2,1)S(1)}, bf16[4,4,32,1024]{3,2,1,0:T(8,128)(2,1)}, u32[]{:S(2)}) copy-start(bf16[4,4,32,1024]{3,2,1,0:T(8,128)(2,1)} %copy-done.6) | copy-start | bytes 3145732
  46.4 13.6 %copy-start = (bf16[6,6,34,1024]{3,2,1,0:T(8,128)(2,1)}, bf16[6,6,34,1024]{3,2,1,0:T(8,128)(2,1)S(1)}, u32[]{:S(2)}) copy-start(bf16[6,6,34,1024]{3,2,1,0:T(8,128)(2,1)S(1)} %pad_maximum_fusion.1.framed) | copy-start | bytes 7520260
  46.4 82.3 %all-to-all-start.1 = ((bf16[64,192,128]{2,1,0:T(8,128)(2,1)}), bf16[64,192,128]{2,1,0:T(8,128)(2,1)}, u32[]{:S(2)}, u32[]{:S(2)}) async-start(bf16[64,192,128]{2,1,0:T(8,128)(2,1)} %gather_pairs.2), calls=%async_computation.1 | async-start | bytes 6291456 | tf_op jit(solution)/shard_map/all_to_all | solution.py:560
  128.7 90.6 %all-to-all-start.2 = ((bf16[64,224,128]{2,1,0:T(8,128)(2,1)}), bf16[64,224,128]{2,1,0:T(8,128)(2,1)}, u32[]{:S(2)}, u32[]{:S(2)}) async-start(bf16[64,224,128]{2,1,0:T(8,128)(2,1)} %gather_pairs.3), calls=%async_computation.2 | async-start | bytes 7340032 | tf_op jit(solution)/shard_map/all_to_all | solution.py:560
  224.6 81.9 %all-to-all-start.3 = ((bf16[64,200,128]{2,1,0:T(8,128)(2,1)}), bf16[64,200,128]{2,1,0:T(8,128)(2,1)S(1)}, u32[]{:S(2)}, u32[]{:S(2)}) async-start(bf16[64,200,128]{2,1,0:T(8,128)(2,1)} %coarse_head.1), calls=%async_computation.3 | async-start | bytes 6553600 | tf_op jit(solution)/shard_map/all_to_all | solution.py:560
  317.4 14.6 %copy-start.2 = (f32[4,4,32,1024]{3,2,1,0:T(8,128)S(1)}, f32[4,4,32,1024]{3,2,1,0:T(8,128)}, u32[]{:S(2)}) copy-start(f32[4,4,32,1024]{3,2,1,0:T(8,128)} %collect.2.grad) | copy-start | bytes 6291460
  317.4 13.4 %collective-permute-start.7 = (bf16[2,4,32,1024]{3,2,1,0:T(8,128)(2,1)S(1)}, bf16[2,4,32,1024]{3,2,1,0:T(8,128)(2,1)}, u32[]{:S(2)}, u32[]{:S(2)}) collective-permute-start(bf16[2,4,32,1024]{3,2,1,0:T(8,128)(2,1)S(1)} %slice.458), channel_id=1, source_target_pairs={{0,56},{1,57},{2,58},{3,59},{4,60},{5,61},{6,62},{7,63},{8,0},{9,1... | collective-permute-start | bytes 1572872 | tf_op jit(solution)/shard_map/ppermute | solution.py:459
  319.0 5.9 %collective-permute-start.6 = (bf16[2,4,1,1024]{3,2,1,0:T(2,128)(2,1)S(1)}, bf16[2,4,1,1024]{3,2,1,0:T(2,128)(2,1)S(1)}, u32[]{:S(2)}, u32[]{:S(2)}) collective-permute-start(bf16[2,4,1,1024]{3,2,1,0:T(2,128)(2,1)S(1)} %slice.457), channel_id=1, source_target_pairs={{0,24},{1,25},{2,26},{3,27},{4,28},{5,29},{6,30},{7,31},{8,32},{9,... | collective-permute-start | bytes 49160 | tf_op jit(solution)/shard_map/ppermute | solution.py:459
  319.1 10.5 %collective-permute-start.5 = (bf16[4,4,1,1024]{3,2,1,0:T(2,128)(2,1)S(1)}, bf16[4,4,1,1024]{3,2,1,0:T(2,128)(2,1)S(1)}, u32[]{:S(2)}, u32[]{:S(2)}) collective-permute-start(bf16[4,4,1,1024]{3,2,1,0:T(2,128)(2,1)S(1)} %broadcast_select_fusion.7), channel_id=1, source_target_pairs={{0,32},{1,33},{2,34},{3,35},{4,36},{5,37},{6,38},{7,39},{8,40},{9,... | collective-permute-start | bytes 98312 | tf_op jit(solution)/shard_map/ppermute | solution.py:459
  333.2 21.6 %copy-start.14 = (bf16[6,1,34,1024]{3,2,1,0:T(8,128)(2,1)S(1)}, bf16[6,1,34,1024]{3,2,1,0:T(8,128)(2,1)}, u32[]{:S(2)}) copy-start(bf16[6,1,34,1024]{3,2,1,0:T(8,128)(2,1)} %get-tuple-element.45) | copy-start | bytes 1253380
  333.2 35.2 %collective-permute-start.8 = (bf16[6,1,34,1024]{3,2,1,0:T(8,128)(2,1)}, bf16[6,1,34,1024]{3,2,1,0:T(8,128)(2,1)S(1)}, u32[]{:S(2)}, u32[]{:S(2)}) collective-permute-start(bf16[6,1,34,1024]{3,2,1,0:T(8,128)(2,1)} %get-tuple-element.44), channel_id=1, source_target_pairs={{0,1},{1,2},{2,3},{3,4},{4,5},{5,6},{6,7},{7,8},{8,9},{9,10},{10,1... | collective-permute-start | bytes 1253384 | tf_op jit(solution)/shard_map/ppermute | solution.py:459
  344.7 21.1 %all-to-all-start.4 = ((f32[64,4,128]{2,1,0:T(4,128)}), f32[64,4,128]{2,1,0:T(4,128)S(1)}, u32[]{:S(2)}, u32[]{:S(2)}) async-start(f32[64,4,128]{2,1,0:T(4,128)} %bitcast.120), calls=%async_computation.4 | async-start | bytes 262144 | tf_op jit(solution)/shard_map/all_to_all | solution.py:560
  354.8 13.7 %collective-permute-start.9 = (bf16[6,1,34,1024]{3,2,1,0:T(8,128)(2,1)S(1)}, bf16[6,1,34,1024]{3,2,1,0:T(8,128)(2,1)S(1)}, u32[]{:S(2)}, u32[]{:S(2)}) collective-permute-start(bf16[6,1,34,1024]{3,2,1,0:T(8,128)(2,1)S(1)} %copy-done.14), channel_id=1, source_target_pairs={{0,63},{1,0},{2,1},{3,2},{4,3},{5,4},{6,5},{7,6},{8,7},{9,8},{10,9... | collective-permute-start | bytes 1253384 | tf_op jit(solution)/shard_map/ppermute | solution.py:459
  373.0 11.8 %slice-start = ((s8[5898240]{0:T(1024)(128)(4,1)}), s8[1703936]{0:T(1024)(128)(4,1)S(1)}, s32[]{:S(2)}) async-start(s8[5898240]{0:T(1024)(128)(4,1)} %bitcast.114), calls=%async_computation.6 | async-start | bytes 3407872
  373.0 80.9 %all-to-all-start.5 = ((bf16[64,200,128]{2,1,0:T(8,128)(2,1)}), bf16[64,200,128]{2,1,0:T(8,128)(2,1)}, u32[]{:S(2)}, u32[]{:S(2)}) async-start(bf16[64,200,128]{2,1,0:T(8,128)(2,1)} %sum_taps.1), calls=%async_computation.5 | async-start | bytes 6553600 | tf_op jit(solution)/shard_map/all_to_all | solution.py:560
  (11 other events, 39.3 us)
